TPU v7x, 32 devices: a whole 2x2x4 slice. The times are simulated.
32 devices in a mesh: tiles: 2 (over y), row: 8 (over z, x), col: 2 (over core).
Axes of the slice: x: 2, y: 2, z: 4, core: 2. Of those that a mesh axis runs over, the one named last changes fastest.
Arguments:
- layers: float32 [8, 4096, 4096], P('tiles', 'row', 'col'), parts along dimension 0, may hold values from -6 to 6
- unmixing: bfloat16 [4, 4, 4, 2048, 4096], P('tiles', None, None, ('row', 'col')), parts along dimension 0, may hold values from -2 to 2
Outputs:
- components: float32 [8, 4096, 4096], P('tiles', 'row', 'col'), parts along dimension 0
There are 2 independent parts, one for each index of `tiles`. A program takes and returns all parts, laid end to end along the dimension named above; each array names one. Nothing has to cross between parts.
All inputs are finite; a program needn't handle non-finite values.
Results may differ from a plain program's by a relative error of at most 0.0003.
Values sent between devices are 32-bit elements; how exact they have to be, the bound alone decides.
No kernel may reach another device: no remote copies, remote signals or barrier semaphores. Data moves between devices by JAX's collectives and lax.ppermute only.
A program may use at most 320 MiB of HBM per device.

v0:
```python
import math

import jax
import jax.numpy as jnp
from jax import lax
from jax.sharding import PartitionSpec as P


def phase_pair(first_len, second_len, period, sign):
    first = lax.broadcasted_iota(jnp.int32, (first_len, second_len), 0)
    second = lax.broadcasted_iota(jnp.int32, (first_len, second_len), 1)
    turns = (first * second % period).astype(jnp.float32)
    phase = turns * (sign * 2.0 * math.pi / period)
    return (jnp.cos(phase), jnp.sin(phase))


def contract_first(values, table):
    return jnp.einsum("...qp,qk->...pk", values, table, precision=lax.Precision.HIGHEST)


def contract_second(values, table):
    return jnp.einsum("...pk,pj->...jk", values, table, precision=lax.Precision.HIGHEST)


def fourier(real_in, imag_in, length, sign, in_len, out_len, real_only):
    inner_len = min(length, 128)
    outer_len = length // inner_len
    rows_in = in_len // outer_len
    rows_out = out_len // inner_len
    leading = real_in.shape[:-1]
    first_cos, first_sin = phase_pair(rows_in, inner_len, inner_len, sign)
    first_table = jnp.concatenate([first_cos, first_sin], axis=1)
    both = contract_first(real_in.reshape(leading + (rows_in, outer_len)), first_table)
    part_real = both[..., :inner_len]
    part_imag = both[..., inner_len:]
    if imag_in is not None:
        other = contract_first(imag_in.reshape(leading + (rows_in, outer_len)), first_table)
        part_real = part_real - other[..., inner_len:]
        part_imag = part_imag + other[..., :inner_len]
    twist_cos, twist_sin = phase_pair(outer_len, inner_len, length, sign)
    turned_real = part_real * twist_cos - part_imag * twist_sin
    turned_imag = part_real * twist_sin + part_imag * twist_cos
    stacked = jnp.concatenate([turned_real, turned_imag], axis=-2)
    second_cos, second_sin = phase_pair(outer_len, rows_out, outer_len, sign)
    table_real = jnp.concatenate([second_cos, -second_sin], axis=0)
    if real_only:
        result_real = contract_second(stacked, table_real)
        return result_real.reshape(leading + (out_len,))
    table_imag = jnp.concatenate([second_sin, second_cos], axis=0)
    combined = contract_second(stacked, jnp.concatenate([table_real, table_imag], axis=1))
    result_real = combined[..., :rows_out, :].reshape(leading + (out_len,))
    result_imag = combined[..., rows_out:, :].reshape(leading + (out_len,))
    return (result_real, result_imag)


def reorder_blocks(values, row_count, col_count):
    leading = values.shape[0]
    block = values.shape[1] // (row_count * col_count)
    width = values.shape[2]
    split = values.reshape(leading, col_count, row_count, block, width)
    return jnp.transpose(split, (0, 4, 2, 1, 3)).reshape(
        leading, width, row_count * col_count * block
    )


def shards(layers, unmixing):
    row_count = lax.axis_size("row")
    col_count = lax.axis_size("col")
    rows_len = layers.shape[1] * row_count
    cols_len = layers.shape[2] * col_count
    spec_real, spec_imag = fourier(
        lax.all_to_all(layers, "col", split_axis=1, concat_axis=2, tiled=True),
        None,
        cols_len,
        -1.0,
        cols_len,
        cols_len // 2,
        False,
    )
    moved_real, moved_imag = (
        lax.all_to_all(
            lax.all_to_all(spec_real, "row", split_axis=2, concat_axis=1, tiled=True),
            "col",
            split_axis=2,
            concat_axis=1,
            tiled=True,
        ),
        lax.all_to_all(
            lax.all_to_all(spec_imag, "row", split_axis=2, concat_axis=1, tiled=True),
            "col",
            split_axis=2,
            concat_axis=1,
            tiled=True,
        ),
    )
    line_real = reorder_blocks(moved_real, row_count, col_count)
    line_imag = reorder_blocks(moved_imag, row_count, col_count)
    wave_real, wave_imag = fourier(line_real, line_imag, rows_len, -1.0, rows_len, rows_len, False)
    mixed_real = None
    mixed_imag = None
    for layer_index in range(4):
        weight_real = unmixing[0, :, layer_index].astype(jnp.float32)
        weight_imag = unmixing[1, :, layer_index].astype(jnp.float32)
        layer_real = wave_real[layer_index][None]
        layer_imag = wave_imag[layer_index][None]
        term_real = weight_real * layer_real - weight_imag * layer_imag
        term_imag = weight_real * layer_imag + weight_imag * layer_real
        if mixed_real is None:
            mixed_real = term_real
            mixed_imag = term_imag
        else:
            mixed_real = mixed_real + term_real
            mixed_imag = mixed_imag + term_imag
    back_real, back_imag = fourier(mixed_real, mixed_imag, rows_len, 1.0, rows_len, rows_len, False)
    scale = 2.0 / (rows_len * cols_len)
    sent_real, sent_imag = (
        lax.all_to_all(
            lax.all_to_all(back_real, "row", split_axis=2, concat_axis=1, tiled=True),
            "col",
            split_axis=2,
            concat_axis=1,
            tiled=True,
        ),
        lax.all_to_all(
            lax.all_to_all(back_imag, "row", split_axis=2, concat_axis=1, tiled=True),
            "col",
            split_axis=2,
            concat_axis=1,
            tiled=True,
        ),
    )
    grid_real = reorder_blocks(sent_real, row_count, col_count)
    grid_imag = reorder_blocks(sent_imag, row_count, col_count)
    fields = fourier(grid_real, grid_imag, cols_len, 1.0, cols_len // 2, cols_len, True)
    fields = fields * scale
    return lax.all_to_all(fields, "col", split_axis=2, concat_axis=1, tiled=True)


def solution(mesh):
    in_specs = (P("tiles", "row", "col"), P("tiles", None, None, ("row", "col"), None))
    out_specs = P("tiles", "row", "col")
    return jax.shard_map(shards, mesh=mesh, in_specs=in_specs, out_specs=out_specs, check_vma=False)
```

profile of v0, /device:TPU:17, one launch (start us, length us, event | category | flops | bytes accessed | tf_op | source)
XLA Modules:
  0.0 1687.2 jit_solution(6777798758830967953)
XLA Ops:
  0.0 20.9 %copy.174 = f32[4,512,2048]{2,0,1:T(4,128)} copy(f32[4,512,2048]{2,1,0:T(8,128)} %param.2) | data formatting | bytes 33554432 | tf_op args[0]
  44.4 17.8 %copy.175 = f32[4,512,2048]{2,1,0:T(8,128)} copy(f32[4,512,2048]{2,0,1:T(4,128)} %all-to-all-done) | data formatting | bytes 33554432 | tf_op jit(solution)/shard_map/all_to_all | solution.py:72
  62.2 16.4 copy.176
  78.6 44.1 %fusion.8 = f32[4,256,32,256]{1,3,2,0:T(8,128)} fusion(f32[4,256,128,32]{1,3,2,0:T(8,128)} %bitcast.134, f32[128,128]{0,1:T(8,128)S(1)} %get-tuple-element.35, f32[128,128]{0,1:T(8,128)S(1)} %get-tuple-element.36), kind=kOutput, calls=%fused_computation.19 | convolution fusion | flops 12884934656 | bytes 50462720 | tf_op jit(solution)/shard_map/...qp,qk->...pk/dot_general | solution.py:18
  122.7 17.6 %multiply_subtract_fusion.1 = (f32[4,256,32,128]{1,3,2,0:T(8,128)S(1)}, f32[4,256,32,128]{1,3,2,0:T(8,128)}) fusion(f32[4,256,32,256]{1,3,2,0:T(8,128)} %fusion.8, f32[32,128]{1,0:T(8,128)S(1)} %get-tuple-element.37, f32[32,128]{1,0:T(8,128)S(1)} %get-tuple-element.38), kind=kLoop, calls=%fused_computation.18 | loop fusion | flops 25165824 | bytes 67141632 | tf_op jit(solution)/shard_map/sub | solution.py:41
  140.3 18.5 %pad_maximum_fusion = f32[4,256,64,128]{1,3,2,0:T(8,128)} fusion(f32[4,256,32,128]{1,3,2,0:T(8,128)} %get-tuple-element.14, f32[4,256,32,128]{1,3,2,0:T(8,128)S(1)} %get-tuple-element.13), kind=kLoop, calls=%fused_computation | loop fusion | flops 8388608 | bytes 67108864 | tf_op jit(solution)/shard_map/concatenate | solution.py:43
  158.8 31.8 %copy.178 = f32[4,256,64,128]{3,2,1,0:T(8,128)} copy(f32[4,256,64,128]{1,3,2,0:T(8,128)} %pad_maximum_fusion) | data formatting | bytes 67108864 | tf_op jit(solution)/shard_map/concatenate | solution.py:43
  190.6 24.1 %convolution_bitcast_fusion = f32[4,256,32,128]{3,2,1,0:T(8,128)S(1)} fusion(f32[4,256,64,128]{3,2,1,0:T(8,128)} %copy.178, f32[32,16]{0,1:T(8,128)S(1)} %get-tuple-element.40, f32[32,16]{0,1:T(8,128)S(1)} %get-tuple-element.39, f32[32,16]{0,1:T(8,128)S(1)} %fusion.98), kind=kOutput, calls=%fused_computation.36 | convolution fusion | flops 3221231616 | bytes 50337792 | tf_op jit(solution)/shard_map/...pk,pj->...jk/dot_general | solution.py:22
  243.4 171.5 %all-to-all-done.1 = f32[4,256,2048]{1,0,2:T(4,128)} async-done(((f32[4,256,2048]{1,0,2:T(4,128)}), f32[4,256,2048]{1,0,2:T(4,128)}, u32[]{:S(2)}, u32[]{:S(2)}) %all-to-all-start.1) | async-done | bytes 8388640 | tf_op jit(solution)/shard_map/all_to_all | solution.py:82
  442.3 19.6 %all_to_all.165 = f32[4,2048,256]{1,0,2:T(4,128)} all-to-all(f32[4,2048,256]{1,0,2:T(4,128)} %copy.182), channel_id=1, replica_groups=mesh['tiles'=2,'row'=8,'col'=2] {'col'}, dimensions={2} | all-to-all | bytes 16777216 | tf_op jit(solution)/shard_map/all_to_all | solution.py:81
  470.1 23.0 %fusion.110 = (bf16[1,4,1,128,4096]{4,3,2,1,0:T(8,128)(2,1)}, bf16[1,4,1,128,4096]{4,3,2,1,0:T(8,128)(2,1)}, bf16[1,4,1,128,4096]{4,3,2,1,0:T(8,128)(2,1)}, bf16...) fusion(bf16[2,4,4,128,4096]{4,3,2,1,0:T(8,128)(2,1)} %param.3), kind=kLoop, calls=%fused_computation.172 | loop fusion | bytes 67108864 | tf_op jit(solution)/shard_map/slice | solution.py:103
  570.7 19.7 %fusion.43 = f32[4,128,32,256]{3,1,2,0:T(8,128)} fusion(f32[4,128,128,32]{1,3,2,0:T(8,128)S(1)} %bitcast.133, f32[128,128]{0,1:T(8,128)S(1)} %copy-done.1, f32[128,128]{0,1:T(8,128)S(1)} %copy-done.3), kind=kOutput, calls=%fused_computation.67 | convolution fusion | flops 6442483712 | bytes 25296896 | tf_op jit(solution)/shard_map/...qp,qk->...pk/dot_general | solution.py:18
  590.3 59.5 %all-to-all-done.3 = f32[4,256,2048]{1,0,2:T(4,128)} async-done(((f32[4,256,2048]{1,0,2:T(4,128)}), f32[4,256,2048]{1,0,2:T(4,128)}, u32[]{:S(2)}, u32[]{:S(2)}) %all-to-all-start.3) | async-done | bytes 8388640 | tf_op jit(solution)/shard_map/all_to_all | solution.py:89
  711.5 19.5 %fusion.41 = f32[4,128,32,256]{3,1,2,0:T(8,128)} fusion(f32[4,128,128,32]{1,3,2,0:T(8,128)S(1)} %bitcast.132, f32[128,128]{0,1:T(8,128)S(1)} %copy-done.1, f32[128,128]{0,1:T(8,128)S(1)} %copy-done.3), kind=kOutput, calls=%fused_computation.65 | convolution fusion | flops 6442483712 | bytes 25296896 | tf_op jit(solution)/shard_map/...qp,qk->...pk/dot_general | solution.py:18
  731.0 19.1 %multiply_subtract_fusion.3 = (f32[4,128,32,128]{3,1,2,0:T(8,128)}, f32[4,128,32,128]{3,1,2,0:T(8,128)}) fusion(f32[32,128]{1,0:T(8,128)S(1)} %copy-done.11, f32[32,128]{1,0:T(8,128)S(1)} %copy-done.13, f32[4,128,32,256]{3,1,2,0:T(8,128)} %fusion.41, f32[4,128,32,256]{3,1,2,0:T(8,128)} %fusion.43), kind=kLoop, calls=%fused_computation.72 | loop fusion | flops 16777216 | bytes 50364416 | tf_op jit(solution)/shard_map/sub | solution.py:41
  762.0 33.5 %fusion.11 = f32[4,128,64,128]{3,2,1,0:T(8,128)} fusion(f32[4,128,64,128]{3,1,2,0:T(8,128)} %pad_maximum_fusion.2, f32[32,32]{0,1:T(8,128)S(1)} %get-tuple-element.42, f32[32,32]{0,1:T(8,128)S(1)} %get-tuple-element.41, f32[32,32]{0,1:T(8,128)S(1)} %fusion.95), kind=kOutput, calls=%fused_computation.37 | convolution fusion | flops 3221237760 | bytes 33566720 | tf_op jit(solution)/shard_map/...pk,pj->...jk/dot_general | solution.py:22
  830.7 17.6 %fusion.22 = (f32[4,128,128,32]{1,3,2,0:T(8,128)S(1)}, f32[4,128,128,32]{1,3,2,0:T(8,128)S(1)}) fusion(bf16[4,128,128,32]{1,3,2,0:T(8,128)(2,1)} %bitcast.169, bf16[4,128,128,32]{1,3,2,0:T(8,128)(2,1)} %bitcast.168, bf16[4,128,128,32]{1,3,2,0:T(8,128)(2,1)} %bitcast.167, bf16[4,128,128,32]{1,3,2,0:T(8,128)(2,1)} %bitcast.166, ...), kind=kLoop, calls=%fused_computation.42 | loop fusion | flops 79691776 | bytes 67108864 | tf_op jit(solution)/shard_map/add | solution.py:112
  848.3 19.4 %fusion.39 = f32[4,128,32,256]{3,1,2,0:T(8,128)} fusion(f32[4,128,128,32]{1,3,2,0:T(8,128)S(1)} %get-tuple-element.7, f32[128,128]{0,1:T(8,128)S(1)} %get-tuple-element.43, f32[128,128]{0,1:T(8,128)S(1)} %get-tuple-element.44), kind=kOutput, calls=%fused_computation.63 | convolution fusion | flops 6442483712 | bytes 25296896 | tf_op jit(solution)/shard_map/...qp,qk->...pk/dot_general | solution.py:18
  867.8 19.5 %fusion.37 = f32[4,128,32,256]{3,1,2,0:T(8,128)} fusion(f32[4,128,128,32]{1,3,2,0:T(8,128)S(1)} %get-tuple-element.8, f32[128,128]{0,1:T(8,128)S(1)} %get-tuple-element.43, f32[128,128]{0,1:T(8,128)S(1)} %get-tuple-element.44), kind=kOutput, calls=%fused_computation.61 | convolution fusion | flops 6442483712 | bytes 25296896 | tf_op jit(solution)/shard_map/...qp,qk->...pk/dot_general | solution.py:18
  887.3 19.1 %multiply_subtract_fusion.2 = (f32[4,128,32,128]{3,1,2,0:T(8,128)}, f32[4,128,32,128]{3,1,2,0:T(8,128)}) fusion(f32[32,128]{1,0:T(8,128)S(1)} %copy-done.8, f32[32,128]{1,0:T(8,128)S(1)} %copy-done.9, f32[4,128,32,256]{3,1,2,0:T(8,128)} %fusion.37, f32[4,128,32,256]{3,1,2,0:T(8,128)} %fusion.39), kind=kLoop, calls=%fused_computation.70 | loop fusion | flops 16777216 | bytes 50364416 | tf_op jit(solution)/shard_map/sub | solution.py:41
  918.3 33.5 %fusion.14 = f32[4,128,64,128]{3,2,1,0:T(8,128)} fusion(f32[4,128,64,128]{3,1,2,0:T(8,128)} %pad_maximum_fusion.3, f32[32,32]{0,1:T(8,128)S(1)} %copy-done.6, f32[32,32]{0,1:T(8,128)S(1)} %copy-done.14, f32[32,32]{0,1:T(8,128)S(1)} %copy-done.4), kind=kOutput, calls=%fused_computation.38 | convolution fusion | flops 3221237760 | bytes 33566720 | tf_op jit(solution)/shard_map/...pk,pj->...jk/dot_general | solution.py:22
  986.7 171.9 %all-to-all-done.5 = f32[4,128,4096]{1,0,2:T(4,128)} async-done(((f32[4,128,4096]{1,0,2:T(4,128)}), f32[4,128,4096]{1,0,2:T(4,128)}, u32[]{:S(2)}, u32[]{:S(2)}) %all-to-all-start.5) | async-done | bytes 8388640 | tf_op jit(solution)/shard_map/all_to_all | solution.py:118
  1184.9 19.3 %all_to_all.167 = f32[4,1024,512]{1,0,2:T(4,128)} all-to-all(f32[4,1024,512]{1,0,2:T(4,128)} %copy.221), channel_id=1, replica_groups=mesh['tiles'=2,'row'=8,'col'=2] {'col'}, dimensions={2} | all-to-all | bytes 16777216 | tf_op jit(solution)/shard_map/all_to_all | solution.py:117
  1240.2 151.8 %all-to-all-done.7 = f32[4,128,4096]{1,0,2:T(4,128)} async-done(((f32[4,128,4096]{1,0,2:T(4,128)}), f32[4,128,4096]{1,0,2:T(4,128)}, u32[]{:S(2)}, u32[]{:S(2)}) %all-to-all-start.7) | async-done | bytes 8388640 | tf_op jit(solution)/shard_map/all_to_all | solution.py:125
  1452.6 31.3 %fusion.33 = f32[4,256,32,256]{3,1,2,0:T(8,128)} fusion(f32[4,256,64,32]{1,3,2,0:T(8,128)S(1)} %bitcast.141, f32[64,128]{1,0:T(8,128)S(1)} %get-tuple-element.49, f32[64,128]{1,0:T(8,128)S(1)} %get-tuple-element.50), kind=kOutput, calls=%fused_computation.57 | convolution fusion | flops 6442467328 | bytes 42008576 | tf_op jit(solution)/shard_map/...qp,qk->...pk/dot_general | solution.py:18
  1483.9 31.5 %fusion.35 = f32[4,256,32,256]{3,1,2,0:T(8,128)} fusion(f32[4,256,64,32]{1,3,2,0:T(8,128)S(1)} %bitcast.140, f32[64,128]{1,0:T(8,128)S(1)} %get-tuple-element.49, f32[64,128]{1,0:T(8,128)S(1)} %get-tuple-element.50), kind=kOutput, calls=%fused_computation.59 | convolution fusion | flops 6442467328 | bytes 42008576 | tf_op jit(solution)/shard_map/...qp,qk->...pk/dot_general | solution.py:18
  1515.4 34.7 %multiply_subtract_fusion = (f32[4,256,32,128]{3,1,2,0:T(8,128)}, f32[4,256,32,128]{3,1,2,0:T(8,128)}) fusion(f32[32,128]{1,0:T(8,128)S(1)} %copy-done.8, f32[32,128]{1,0:T(8,128)S(1)} %copy-done.9, f32[4,256,32,256]{3,1,2,0:T(8,128)} %fusion.33, f32[4,256,32,256]{3,1,2,0:T(8,128)} %fusion.35), kind=kLoop, calls=%fused_computation.16 | loop fusion | flops 33554432 | bytes 100696064 | tf_op jit(solution)/shard_map/sub | solution.py:41
  1550.1 23.3 %pad_maximum_fusion.1 = f32[4,256,64,128]{3,1,2,0:T(8,128)} fusion(f32[4,256,32,128]{3,1,2,0:T(8,128)} %get-tuple-element.6, f32[4,256,32,128]{3,1,2,0:T(8,128)} %get-tuple-element.5), kind=kLoop, calls=%fused_computation.1 | loop fusion | flops 8388608 | bytes 67108864 | tf_op jit(solution)/shard_map/concatenate | solution.py:43
  1573.4 47.1 %multiply_bitcast_fusion = f32[4,256,32,128]{3,2,1,0:T(8,128)} fusion(f32[4,256,64,128]{3,1,2,0:T(8,128)} %pad_maximum_fusion.1, f32[32,32]{0,1:T(8,128)S(1)} %copy-done.5, f32[32,32]{0,1:T(8,128)S(1)} %copy-done.7), kind=kOutput, calls=%fused_computation.14 | convolution fusion | flops 3225421824 | bytes 50339840 | tf_op jit(solution)/shard_map/...pk,pj->...jk/dot_general | solution.py:22
  1620.5 15.5 copy.255
  1636.0 31.6 %all_to_all.169 = f32[4,256,4096]{1,0,2:T(4,128)} all-to-all(f32[4,256,4096]{1,0,2:T(4,128)} %bitcast.136), channel_id=1, replica_groups=mesh['tiles'=2,'row'=8,'col'=2] {'col'}, dimensions={2} | all-to-all | bytes 33554432 | tf_op jit(solution)/shard_map/all_to_all | solution.py:136
  1667.6 19.2 %copy.236 = f32[4,2,256,2048]{3,2,1,0:T(8,128)} copy(f32[4,2,256,2048]{2,0,3,1:T(4,128)} %bitcast.137) | data formatting | bytes 33554432 | tf_op jit(solution)/shard_map/all_to_all | solution.py:136
  (103 shorter events, 443.5 us)
Async XLA Ops:
  20.9 23.5 %all-to-all-start = ((f32[4,512,2048]{2,0,1:T(4,128)}), f32[4,512,2048]{2,0,1:T(4,128)}, u32[]{:S(2)}, u32[]{:S(2)}) async-start(f32[4,512,2048]{2,0,1:T(4,128)} %copy.174), calls=%async_computation | async-start | bytes 33554432 | tf_op jit(solution)/shard_map/all_to_all | solution.py:72
  31.5 91.2 %copy-start.10 = (f32[32,128]{1,0:T(8,128)}, f32[32,128]{1,0:T(8,128)S(1)}, u32[]{:S(2)}) copy-start(f32[32,128]{1,0:T(8,128)S(1)} %get-tuple-element.37) | copy-start | bytes 49156
  31.5 91.2 %copy-start.12 = (f32[32,128]{1,0:T(8,128)}, f32[32,128]{1,0:T(8,128)S(1)}, u32[]{:S(2)}) copy-start(f32[32,128]{1,0:T(8,128)S(1)} %get-tuple-element.38) | copy-start | bytes 49156
  31.8 46.8 %copy-start = (f32[128,128]{0,1:T(8,128)}, f32[128,128]{0,1:T(8,128)S(1)}, u32[]{:S(2)}) copy-start(f32[128,128]{0,1:T(8,128)S(1)} %get-tuple-element.35) | copy-start | bytes 196612
  31.8 46.8 %copy-start.2 = (f32[128,128]{0,1:T(8,128)}, f32[128,128]{0,1:T(8,128)S(1)}, u32[]{:S(2)}) copy-start(f32[128,128]{0,1:T(8,128)S(1)} %get-tuple-element.36) | copy-start | bytes 196612
  229.8 185.1 %all-to-all-start.1 = ((f32[4,256,2048]{1,0,2:T(4,128)}), f32[4,256,2048]{1,0,2:T(4,128)}, u32[]{:S(2)}, u32[]{:S(2)}) async-start(f32[4,256,2048]{1,0,2:T(4,128)} %bitcast.144), calls=%async_computation.1 | async-start | bytes 16777216 | tf_op jit(solution)/shard_map/all_to_all | solution.py:82
  461.9 188.0 %all-to-all-start.3 = ((f32[4,256,2048]{1,0,2:T(4,128)}), f32[4,256,2048]{1,0,2:T(4,128)}, u32[]{:S(2)}, u32[]{:S(2)}) async-start(f32[4,256,2048]{1,0,2:T(4,128)} %bitcast.142), calls=%async_computation.3 | async-start | bytes 16777216 | tf_op jit(solution)/shard_map/all_to_all | solution.py:89
  566.7 4.0 copy-start.1
  566.7 4.0 copy-start.3
  711.5 19.6 %copy-start.11 = (f32[32,128]{1,0:T(8,128)S(1)}, f32[32,128]{1,0:T(8,128)}, u32[]{:S(2)}) copy-start(f32[32,128]{1,0:T(8,128)} %copy-done.10) | copy-start | bytes 49156
  711.5 19.6 %copy-start.13 = (f32[32,128]{1,0:T(8,128)S(1)}, f32[32,128]{1,0:T(8,128)}, u32[]{:S(2)}) copy-start(f32[32,128]{1,0:T(8,128)} %copy-done.12) | copy-start | bytes 49156
  867.8 19.5 %copy-start.8 = (f32[32,128]{1,0:T(8,128)S(1)}, f32[32,128]{1,0:T(8,128)}, u32[]{:S(2)}) copy-start(f32[32,128]{1,0:T(8,128)} %get-tuple-element.45) | copy-start | bytes 49156
  867.8 19.5 %copy-start.9 = (f32[32,128]{1,0:T(8,128)S(1)}, f32[32,128]{1,0:T(8,128)}, u32[]{:S(2)}) copy-start(f32[32,128]{1,0:T(8,128)} %get-tuple-element.46) | copy-start | bytes 49156
  906.4 11.9 copy-start.4
  906.4 11.9 copy-start.6
  906.4 11.9 copy-start.14
  970.8 187.8 %all-to-all-start.5 = ((f32[4,128,4096]{1,0,2:T(4,128)}), f32[4,128,4096]{1,0,2:T(4,128)}, u32[]{:S(2)}, u32[]{:S(2)}) async-start(f32[4,128,4096]{1,0,2:T(4,128)} %bitcast.145), calls=%async_computation.5 | async-start | bytes 16777216 | tf_op jit(solution)/shard_map/all_to_all | solution.py:118
  1204.2 187.8 %all-to-all-start.7 = ((f32[4,128,4096]{1,0,2:T(4,128)}), f32[4,128,4096]{1,0,2:T(4,128)}, u32[]{:S(2)}, u32[]{:S(2)}) async-start(f32[4,128,4096]{1,0,2:T(4,128)} %bitcast.143), calls=%async_computation.7 | async-start | bytes 16777216 | tf_op jit(solution)/shard_map/all_to_all | solution.py:125
  1448.4 35.5 %slice-start = ((s8[8388608]{0:T(1024)(128)(4,1)}), s8[4194304]{0:T(1024)(128)(4,1)S(1)}, s32[]{:S(2)}) async-start(s8[8388608]{0:T(1024)(128)(4,1)} %bitcast.138), calls=%async_computation.10 | async-start | bytes 8388608
  1452.5 31.3 %slice-start.1 = ((s8[8388608]{0:T(1024)(128)(4,1)}), s8[4194304]{0:T(1024)(128)(4,1)S(1)}, s32[]{:S(2)}) async-start(s8[8388608]{0:T(1024)(128)(4,1)} %bitcast.138), calls=%async_computation.11 | async-start | bytes 8388608
  1550.1 23.3 %copy-start.5 = (f32[32,32]{0,1:T(8,128)S(1)}, f32[32,32]{0,1:T(8,128)}, u32[]{:S(2)}) copy-start(f32[32,32]{0,1:T(8,128)} %fusion.94) | copy-start | bytes 12292
  1550.1 23.3 %copy-start.7 = (f32[32,32]{0,1:T(8,128)S(1)}, f32[32,32]{0,1:T(8,128)}, u32[]{:S(2)}) copy-start(f32[32,32]{0,1:T(8,128)} %get-tuple-element.48) | copy-start | bytes 12292
where the time goes:
time: 1700 us; the launch traced here: 1690 us
  waiting for transfers between devices  567 us (33%)
  local copies, waits for them, and re-layouts  482 us (28%)
  matrix products  323 us (19%)
  other arithmetic  177 us (10%)
  blocking collectives  96.9 us (6%)
  starting transfers between devices  40.1 us (2%)
    dot_general x7, matrix products, contract_first(): jnp.einsum('...qp,qk->...pk', values, table, precision=lax.Precision.HIGH...  185 us
    all_to_all x1, waiting for transfers between devices, shards(): lax.all_to_all(back_real, 'row', split_axis=2, concat_axis=1, tiled=True)  172 us
    all_to_all x1, waiting for transfers between devices, shards(): lax.all_to_all(spec_real, 'row', split_axis=2, concat_axis=1, tiled=True)  172 us
    all_to_all x1, waiting for transfers between devices, shards(): lax.all_to_all(back_imag, 'row', split_axis=2, concat_axis=1, tiled=True)  152 us
    dot_general x4, matrix products, contract_second(): jnp.einsum('...pk,pj->...jk', values, table, precision=lax.Precision.HIGH...  138 us
    sub x4, other arithmetic, fourier(): turned_real = part_real * twist_cos - part_imag * twist_sin  90.5 us
    unnamed x43, local copies, waits for them, and re-layouts  71.9 us
    concatenate x4, other arithmetic, fourier(): stacked = jnp.concatenate([turned_real, turned_imag], axis=-2)  65.5 us
  transfers between devices with their start and end apart: 5, of which 5 were waited for; matrix products, arithmetic and copies ran while one was open for 10% of the time, Pallas kernels for 0%

commit v1 on v0

--- a/solution.py
+++ b/solution.py
@@ -2,8 +2,488 @@
 
 import jax
 import jax.numpy as jnp
+import ml_dtypes
+import numpy as np
 from jax import lax
+from jax.experimental import pallas as pl
+from jax.experimental.pallas import tpu as pltpu
 from jax.sharding import PartitionSpec as P
+
+RADIX = 16
+
+
+def split_table(table):
+    high = table.astype(ml_dtypes.bfloat16)
+    low = (table - high.astype(np.float64)).astype(ml_dtypes.bfloat16)
+    return np.stack([high, low])
+
+
+def twiddle_table(count, width, length, sign):
+    turns = np.outer(np.arange(count), np.arange(width)) % length
+    phase = turns * (sign * 2.0 * math.pi / length)
+    pair = np.stack([np.cos(phase), np.sin(phase)], axis=1)
+    return np.ascontiguousarray(
+        np.broadcast_to(pair[:, :, None, :], (count, 2, 8, width))
+    ).astype(np.float32)
+
+
+def line_table(out_len, width, sign):
+    turns = np.outer(np.arange(out_len), np.arange(width)) % width
+    phase = turns * (sign * 2.0 * math.pi / width)
+    return split_table(np.concatenate([np.cos(phase), np.sin(phase)], axis=0))
+
+
+def real_table(out_len, width, scale):
+    turns = np.outer(np.arange(out_len), np.arange(width)) % width
+    phase = turns * (2.0 * math.pi / width)
+    return split_table(scale * np.concatenate([np.cos(phase), -np.sin(phase)], axis=1))
+
+
+def turn(value, numerator, denominator):
+    real, imag = value
+    numerator %= denominator
+    eighths = 8 * numerator / denominator
+    if eighths == 0:
+        return (real, imag)
+    if eighths == 2:
+        return (-imag, real)
+    if eighths == 4:
+        return (-real, -imag)
+    if eighths == 6:
+        return (imag, -real)
+    cos = math.cos(2.0 * math.pi * numerator / denominator)
+    sin = math.sin(2.0 * math.pi * numerator / denominator)
+    if eighths in (1, 3, 5, 7):
+        half = math.sqrt(0.5)
+        scaled_sum = (real + imag) * half
+        scaled_gap = (real - imag) * half
+        if eighths == 1:
+            return (scaled_gap, scaled_sum)
+        if eighths == 3:
+            return (-scaled_sum, scaled_gap)
+        if eighths == 5:
+            return (-scaled_gap, -scaled_sum)
+        return (scaled_sum, -scaled_gap)
+    return (real * cos - imag * sin, real * sin + imag * cos)
+
+
+def add(left, right):
+    return (left[0] + right[0], left[1] + right[1])
+
+
+def gap(left, right):
+    return (left[0] - right[0], left[1] - right[1])
+
+
+def small_fourier(values, sign):
+    count = len(values)
+    if count == 1:
+        return values
+    even = small_fourier(values[0::2], sign)
+    odd = small_fourier(values[1::2], sign)
+    odd = [turn(value, sign * index, count) for index, value in enumerate(odd)]
+    return [add(e, o) for e, o in zip(even, odd)] + [gap(e, o) for e, o in zip(even, odd)]
+
+
+def small_real_fourier(values, sign):
+    count = len(values)
+    if count == 2:
+        zero = jnp.zeros_like(values[0])
+        return [(values[0] + values[1], zero), (values[0] - values[1], zero)]
+    even = small_real_fourier(values[0::2], sign)
+    odd = small_real_fourier(values[1::2], sign)
+    result = [None] * count
+    for index in range(count // 4 + 1):
+        turned = turn(odd[index], sign * index, count)
+        upper = add(even[index], turned)
+        lower = gap(even[index], turned)
+        result[index] = upper
+        result[count // 2 - index] = (lower[0], -lower[1])
+    for index in range(1, count // 2):
+        result[count - index] = (result[index][0], -result[index][1])
+    return result
+
+
+def twist(value, table_ref, index, lanes):
+    if index == 0:
+        return value
+    cos = table_ref[index, 0, :, lanes]
+    sin = table_ref[index, 1, :, lanes]
+    return (value[0] * cos - value[1] * sin, value[0] * sin + value[1] * cos)
+
+
+def dot_rows(table, values):
+    return lax.dot_general(
+        table, values, (((1,), (1,)), ((), ())), preferred_element_type=jnp.float32
+    )
+
+
+def matmul_split(table_ref, values):
+    high = values.astype(jnp.bfloat16)
+    low = (values - high.astype(jnp.float32)).astype(jnp.bfloat16)
+    return (
+        dot_rows(table_ref[0], high)
+        + dot_rows(table_ref[0], low)
+        + dot_rows(table_ref[1], high)
+    )
+
+
+def combine(products, out_len, rows):
+    cos_part = products[:out_len]
+    sin_part = products[out_len:]
+    real = cos_part[:, :rows] - sin_part[:, rows:]
+    imag = cos_part[:, rows:] + sin_part[:, :rows]
+    return real, imag
+
+
+def row_forward_kernel(core_ref, own_ref, other_ref, twist_ref, table_ref, out_ref, part_ref):
+    rows = own_ref.shape[1]
+    width = part_ref.shape[2]
+    per_half = RADIX // 2
+
+    def small(step, _):
+        row = pl.multiple_of(step * 8, 8)
+        for lane in range(width // 128):
+            lanes = pl.ds(lane * 128, 128)
+            values = [
+                half_ref[0, pl.ds(row, 8), pl.ds(index * width + lane * 128, 128)]
+                for half_ref in (own_ref, other_ref)
+                for index in range(per_half)
+            ]
+            for index, value in enumerate(small_real_fourier(values, -1)):
+                real, imag = twist(value, twist_ref, index, lanes)
+                part_ref[index, pl.ds(row, 8), lanes] = real
+                part_ref[index, pl.ds(rows + row, 8), lanes] = imag
+        return 0
+
+    lax.fori_loop(0, rows // 8, small, 0)
+    blocks, _, _, per_block, _ = out_ref.shape
+    out_len = blocks * per_block // RADIX
+    piece = per_block // RADIX
+
+    def line(index, _):
+        real, imag = combine(matmul_split(table_ref, part_ref[index]), out_len, rows)
+        for block in range(blocks):
+            place = pl.ds(index, piece, stride=RADIX)
+            out_ref[block, 0, 0, place, :] = real[block * piece : (block + 1) * piece]
+            out_ref[block, 0, 1, place, :] = imag[block * piece : (block + 1) * piece]
+        return 0
+
+    lax.fori_loop(0, RADIX, line, 0)
+
+
+def complex_lines(read, rows, width, sign, twist_ref, part_ref):
+    def small(step, _):
+        row = pl.multiple_of(step * 8, 8)
+        for lane in range(width // 128):
+            lanes = pl.ds(lane * 128, 128)
+            values = [
+                (read(index, 0, pl.ds(row, 8), lanes), read(index, 1, pl.ds(row, 8), lanes))
+                for index in range(RADIX)
+            ]
+            for index, value in enumerate(small_fourier(values, sign)):
+                real, imag = twist(value, twist_ref, index, lanes)
+                part_ref[index, pl.ds(row, 8), lanes] = real
+                part_ref[index, pl.ds(rows + row, 8), lanes] = imag
+        return 0
+
+    lax.fori_loop(0, rows // 8, small, 0)
+
+
+def column_forward_kernel(x_ref, twist_ref, table_ref, out_ref, part_ref, order_ref):
+    rows = x_ref.shape[3]
+    width = x_ref.shape[4]
+
+    def read(index, part, row, lanes):
+        return x_ref[index, 0, part, row, lanes]
+
+    complex_lines(read, rows, width, -1, twist_ref, part_ref)
+
+    def line(index, _):
+        real, imag = combine(matmul_split(table_ref, part_ref[index]), width, rows)
+        order_ref[0, pl.ds(index, width, stride=RADIX), :] = real
+        order_ref[1, pl.ds(index, width, stride=RADIX), :] = imag
+        return 0
+
+    lax.fori_loop(0, RADIX, line, 0)
+
+    def flip(index, _):
+        start = pl.multiple_of(index * width, width)
+        for part in range(2):
+            out_ref[0, part, :, pl.ds(start, width)] = order_ref[part, pl.ds(start, width), :].T
+        return 0
+
+    lax.fori_loop(0, RADIX, flip, 0)
+
+
+def mix_rows(waves, unmix_ref, row, real, imag):
+    for layer, wave in enumerate(waves):
+        weight_real = unmix_ref[0, 0, layer, pl.ds(row, 16), :].astype(jnp.float32)
+        weight_imag = unmix_ref[1, 0, layer, pl.ds(row, 16), :].astype(jnp.float32)
+        wave_real = wave[0, 0, pl.ds(row, 16), :]
+        wave_imag = wave[0, 1, pl.ds(row, 16), :]
+        term_real = weight_real * wave_real - weight_imag * wave_imag
+        term_imag = weight_real * wave_imag + weight_imag * wave_real
+        real = term_real if real is None else real + term_real
+        imag = term_imag if imag is None else imag + term_imag
+    return real, imag
+
+
+def partial_mix_kernel(w0_ref, w1_ref, w2_ref, unmix_ref, out_ref):
+    def mix(block, _):
+        row = pl.multiple_of(block * 16, 16)
+        real, imag = mix_rows((w0_ref, w1_ref, w2_ref), unmix_ref, row, None, None)
+        out_ref[0, 0, pl.ds(row, 16), :] = real
+        out_ref[0, 1, pl.ds(row, 16), :] = imag
+        return 0
+
+    lax.fori_loop(0, out_ref.shape[2] // 16, mix, 0)
+
+
+def column_inverse_kernel(
+    sum_ref, wave_ref, unmix_ref, twist_ref, table_ref, out_ref, mixed_ref, part_ref
+):
+    step = pl.program_id(1)
+    rows = mixed_ref.shape[2]
+    width = mixed_ref.shape[3]
+
+    def mix(block, _):
+        row = pl.multiple_of(block * 16, 16)
+        real, imag = mix_rows(
+            (wave_ref,),
+            unmix_ref,
+            row,
+            sum_ref[0, 0, pl.ds(row, 16), :],
+            sum_ref[0, 1, pl.ds(row, 16), :],
+        )
+        mixed_ref[step, 0, pl.ds(row, 16), :] = real
+        mixed_ref[step, 1, pl.ds(row, 16), :] = imag
+        return 0
+
+    lax.fori_loop(0, rows // 16, mix, 0)
+
+    @pl.when(step == RADIX - 1)
+    def _():
+        def read(index, part, row, lanes):
+            return mixed_ref[index, part, row, lanes]
+
+        complex_lines(read, rows, width, 1, twist_ref, part_ref)
+        blocks, _, _, per_block, _ = out_ref.shape
+        piece = per_block // RADIX
+
+        def line(index, _):
+            real, imag = combine(matmul_split(table_ref, part_ref[index]), width, rows)
+            for block in range(blocks):
+                place = pl.ds(index, piece, stride=RADIX)
+                out_ref[block, 0, 0, place, :] = real[block * piece : (block + 1) * piece]
+                out_ref[block, 0, 1, place, :] = imag[block * piece : (block + 1) * piece]
+            return 0
+
+        lax.fori_loop(0, RADIX, line, 0)
+
+
+def row_inverse_kernel(core_ref, x_ref, twist_ref, table_ref, *refs):
+    out_ref, sent_ref, part_ref, order_ref = refs[-4:]
+    rows = x_ref.shape[3]
+    width = x_ref.shape[4]
+    count = 2 * RADIX
+    lanes = pl.ds(0, width)
+
+    def small(step, _):
+        row = pl.multiple_of(step * 8, 8)
+        for odd in range(2):
+            values = [
+                (x_ref[index, 0, 0, pl.ds(row, 8), :], x_ref[index, 0, 1, pl.ds(row, 8), :])
+                for index in range(RADIX)
+            ]
+            if odd:
+                values = [turn(value, index, count) for index, value in enumerate(values)]
+            for index, value in enumerate(small_fourier(values, 1)):
+                real, imag = twist(value, twist_ref, 2 * index + odd, lanes)
+                part_ref[2 * index + odd, pl.ds(row, 8), pl.ds(0, width)] = real
+                part_ref[2 * index + odd, pl.ds(row, 8), pl.ds(width, width)] = imag
+        return 0
+
+    lax.fori_loop(0, rows // 8, small, 0)
+    out_len = table_ref.shape[1]
+
+    def line(index, _):
+        order_ref[pl.ds(index, out_len, stride=count), :] = matmul_split(table_ref, part_ref[index])
+        return 0
+
+    lax.fori_loop(0, count, line, 0)
+    half_len = sent_ref.shape[1]
+    chunk = 256
+    own = core_ref[0] * half_len
+    other = half_len - own
+
+    def flip(index, _):
+        start = pl.multiple_of(index * chunk, chunk)
+        own_start = pl.multiple_of(own + start, chunk)
+        other_start = pl.multiple_of(other + start, chunk)
+        sent_ref[:, pl.ds(start, chunk)] = order_ref[pl.ds(other_start, chunk), :].T
+        out_ref[0, :, pl.ds(start, chunk)] = order_ref[pl.ds(own_start, chunk), :].T
+        return 0
+
+    lax.fori_loop(0, half_len // chunk, flip, 0)
+
+
+def whole(array):
+    return pl.BlockSpec(array.shape, lambda *_: (0,) * array.ndim)
+
+
+VMEM_LIMIT = 56 * 1024 * 1024
+ROW_TILE = 128
+
+
+def params(rank):
+    return pltpu.CompilerParams(
+        dimension_semantics=("arbitrary",) * rank, vmem_limit_bytes=VMEM_LIMIT
+    )
+
+
+def row_forward(layers, other, core, first, blocks, per_block):
+    count, rows, half_len = other.shape
+    length = 2 * half_len
+    width = length // RADIX
+    tiles = rows // ROW_TILE
+    signs = jnp.where(jnp.arange(RADIX) % 2 == 1, 1.0 - 2.0 * core[0].astype(jnp.float32), 1.0)
+    twists = jnp.asarray(twiddle_table(RADIX, width, length, -1)) * signs[:, None, None, None]
+    table = jnp.asarray(line_table(blocks * per_block // RADIX, width, -1))
+    return pl.pallas_call(
+        row_forward_kernel,
+        grid_spec=pltpu.PrefetchScalarGridSpec(
+            num_scalar_prefetch=1,
+            grid=(count, tiles),
+            in_specs=[
+                pl.BlockSpec(
+                    (1, ROW_TILE, half_len), lambda m, i, c: (first + m, c[0] * tiles + i, 0)
+                ),
+                pl.BlockSpec((1, ROW_TILE, half_len), lambda m, i, c: (m, i, 0)),
+                whole(twists),
+                whole(table),
+            ],
+            out_specs=pl.BlockSpec(
+                (blocks, 1, 2, per_block, ROW_TILE), lambda m, i, c: (0, m, 0, 0, i)
+            ),
+            scratch_shapes=[pltpu.VMEM((RADIX, 2 * ROW_TILE, width), jnp.float32)],
+        ),
+        out_shape=jax.ShapeDtypeStruct((blocks, count, 2, per_block, rows), jnp.float32),
+        compiler_params=params(2),
+        name="row_forward",
+    )(core, layers, other, twists, table)
+
+
+def column_forward(x):
+    blocks, count, _, rows, width = x.shape
+    length = RADIX * width
+    twists = jnp.asarray(twiddle_table(RADIX, width, length, -1))
+    table = jnp.asarray(line_table(width, width, -1))
+    return pl.pallas_call(
+        column_forward_kernel,
+        grid=(count,),
+        in_specs=[
+            pl.BlockSpec((blocks, 1, 2, rows, width), lambda m: (0, m, 0, 0, 0)),
+            whole(twists),
+            whole(table),
+        ],
+        out_specs=pl.BlockSpec((1, 2, rows, length), lambda m: (m, 0, 0, 0)),
+        out_shape=jax.ShapeDtypeStruct((count, 2, rows, length), jnp.float32),
+        scratch_shapes=[
+            pltpu.VMEM((RADIX, 2 * rows, width), jnp.float32),
+            pltpu.VMEM((2, length, rows), jnp.float32),
+        ],
+        compiler_params=params(1),
+        name="column_forward",
+    )(x, twists, table)
+
+
+def partial_mix(waves, unmixing):
+    components = unmixing.shape[1]
+    _, _, rows, length = waves[0][0].shape
+    width = length // RADIX
+
+    def wave_spec(place):
+        return pl.BlockSpec((1, 2, rows, width), lambda i, j: (place, 0, 0, i))
+
+    return pl.pallas_call(
+        partial_mix_kernel,
+        grid=(RADIX, components),
+        in_specs=[wave_spec(place) for _, place in waves]
+        + [pl.BlockSpec((2, 1, len(waves), rows, width), lambda i, j: (0, j, 0, 0, i))],
+        out_specs=pl.BlockSpec((1, 2, rows, width), lambda i, j: (j, 0, 0, i)),
+        out_shape=jax.ShapeDtypeStruct((components, 2, rows, length), jnp.float32),
+        compiler_params=params(2),
+        name="partial_mix",
+    )(*[wave for wave, _ in waves], unmixing)
+
+
+def column_inverse(sums, wave, place, layer, unmixing, first, count, blocks):
+    _, _, rows, length = sums.shape
+    width = length // RADIX
+    per_block = length // blocks
+    twists = jnp.asarray(twiddle_table(RADIX, width, length, 1))
+    table = jnp.asarray(line_table(width, width, 1))
+    return pl.pallas_call(
+        column_inverse_kernel,
+        grid=(count, RADIX),
+        in_specs=[
+            pl.BlockSpec((1, 2, rows, width), lambda j, i: (first + j, 0, 0, i)),
+            pl.BlockSpec((1, 2, rows, width), lambda j, i: (place, 0, 0, i)),
+            pl.BlockSpec((2, 1, 1, rows, width), lambda j, i: (0, first + j, layer, 0, i)),
+            whole(twists),
+            whole(table),
+        ],
+        out_specs=pl.BlockSpec((blocks, 1, 2, per_block, rows), lambda j, i: (0, j, 0, 0, 0)),
+        out_shape=jax.ShapeDtypeStruct((blocks, count, 2, per_block, rows), jnp.float32),
+        scratch_shapes=[
+            pltpu.VMEM((RADIX, 2, rows, width), jnp.float32),
+            pltpu.VMEM((RADIX, 2 * rows, width), jnp.float32),
+        ],
+        compiler_params=params(2),
+        name="column_inverse",
+    )(sums, wave, unmixing, twists, table)
+
+
+def row_inverse(x, place, component, shape, fields, core, scale):
+    blocks, _, _, rows, width = x.shape
+    half_len = shape[2]
+    length = 2 * half_len
+    count = 2 * RADIX
+    tiles = rows // ROW_TILE
+    twists = jnp.asarray(twiddle_table(count, width, length, 1))
+    table = jnp.asarray(real_table(length // count, width, scale))
+    held = [] if fields is None else [fields]
+    return pl.pallas_call(
+        row_inverse_kernel,
+        grid_spec=pltpu.PrefetchScalarGridSpec(
+            num_scalar_prefetch=1,
+            grid=(tiles,),
+            in_specs=[
+                pl.BlockSpec((blocks, 1, 2, ROW_TILE, width), lambda i, c: (0, place, 0, i, 0)),
+                whole(twists),
+                whole(table),
+            ]
+            + [pl.BlockSpec(memory_space=pl.ANY)] * len(held),
+            out_specs=[
+                pl.BlockSpec(
+                    (1, ROW_TILE, half_len), lambda i, c: (component, c[0] * tiles + i, 0)
+                ),
+                pl.BlockSpec((ROW_TILE, half_len), lambda i, c: (i, 0)),
+            ],
+            scratch_shapes=[
+                pltpu.VMEM((count, ROW_TILE, 2 * width), jnp.float32),
+                pltpu.VMEM((length, ROW_TILE), jnp.float32),
+            ],
+        ),
+        out_shape=[
+            jax.ShapeDtypeStruct(shape, jnp.float32),
+            jax.ShapeDtypeStruct((rows, half_len), jnp.float32),
+        ],
+        input_output_aliases={4: 0} if held else {},
+        compiler_params=params(1),
+        name="row_inverse",
+    )(core, x, twists, table, *held)
 
 
 def phase_pair(first_len, second_len, period, sign):
@@ -63,7 +543,7 @@
     )
 
 
-def shards(layers, unmixing):
+def general_shards(layers, unmixing):
     row_count = lax.axis_size("row")
     col_count = lax.axis_size("col")
     rows_len = layers.shape[1] * row_count
@@ -136,6 +616,67 @@
     return lax.all_to_all(fields, "col", split_axis=2, concat_axis=1, tiled=True)
 
 
+def swap_cores(values):
+    return lax.ppermute(values, "col", [(0, 1), (1, 0)])
+
+
+def exchange(values):
+    return lax.all_to_all(values, ("row", "col"), split_axis=0, concat_axis=0, tiled=True)
+
+
+def layer_shards(layers, unmixing):
+    row_count = lax.axis_size("row")
+    col_count = lax.axis_size("col")
+    blocks = row_count * col_count
+    _, block_rows, half_len = layers.shape
+    rows = block_rows // col_count
+    per_block = unmixing.shape[3]
+    core = lax.axis_index("col").astype(jnp.int32).reshape(1)
+    own_row = core[0] * rows
+    other_row = rows - own_row
+    groups = ((0, 1), (1, 2), (3, 1))
+
+    source = layers
+    moved = None
+    arrived = []
+    for first, count in groups:
+        given = lax.dynamic_slice(source, (first, other_row, 0), (count, rows, half_len))
+        spectra = row_forward(layers, swap_cores(given), core, first, blocks, per_block)
+        source, spectra = lax.optimization_barrier((source, spectra))
+        if moved is not None:
+            spectra, moved = lax.optimization_barrier((spectra, moved))
+        moved = exchange(spectra)
+        arrived.append(moved)
+    waves = []
+    for (_, count), moved in zip(groups, arrived):
+        group = column_forward(moved)
+        waves += [(group, place) for place in range(count)]
+    sums = partial_mix(waves[:3], unmixing)
+    scale = 2.0 / (block_rows * row_count * half_len * col_count)
+    fields = None
+    for first, count in groups:
+        back = column_inverse(sums, *waves[3], 3, unmixing, first, count, blocks)
+        if first > 0:
+            back, sent = lax.optimization_barrier((back, sent))
+        sent = exchange(back)
+        for place in range(count):
+            fields, given = row_inverse(
+                sent, place, first + place, layers.shape, fields, core, scale
+            )
+            taken = swap_cores(given)[None]
+            fields = lax.dynamic_update_slice(fields, taken, (first + place, other_row, 0))
+    return fields
+
+
+def shards(layers, unmixing):
+    col_count = lax.axis_size("col")
+    blocks = lax.axis_size("row") * col_count
+    shape = (blocks, col_count) + layers.shape + unmixing.shape[1:]
+    if shape == (RADIX, 2, 4, 512, 2048, 4, 4, 128, 4096):
+        return layer_shards(layers, unmixing)
+    return general_shards(layers, unmixing)
+
+
 def solution(mesh):
     in_specs = (P("tiles", "row", "col"), P("tiles", None, None, ("row", "col"), None))
     out_specs = P("tiles", "row", "col")

time: 1700 us -> 862 us (0.51)
  local copies, waits for them, and re-layouts: 482 us -> 17.9 us
  Pallas kernels: 0 us -> 356 us
  matrix products: 323 us -> 0 us
  other arithmetic: 177 us -> 0.8 us
  waiting for transfers between devices: 567 us -> 449 us
  blocking collectives: 96.9 us -> 0 us
    pallas_call x0 -> x14, Pallas kernels: none -> 356 us  [the longest x4 102 us: row_inverse(): pl.pallas_call(row_inverse_kernel, grid_spec=pltpu.PrefetchScalarGridSpec...]
    dot_general x11 -> x0, matrix products: 323 us -> none  [the longest x7 185 us: contract_first(): jnp.einsum('...qp,qk->...pk', values, table, precision=lax.Precision.HIGH...]
    all_to_all x23 -> x0, local copies, waits for them, and re-layouts: 235 us -> none  [the longest x2 34.2 us: shards(): lax.all_to_all(layers, 'col', split_axis=1, concat_axis=2, tiled=True)]
    all_to_all x5 -> x6, waiting for transfers between devices: 567 us -> 423 us  [exchange(): lax.all_to_all(values, ('row', 'col'), split_axis=0, concat_axis=0, tiled...]
    all_to_all x5 -> x0, blocking collectives: 96.9 us -> none  [the longest x1 31.6 us: shards(): lax.all_to_all(fields, 'col', split_axis=2, concat_axis=1, tiled=True)]
    sub x4 -> x0, other arithmetic: 90.5 us -> none  [fourier(): turned_real = part_real * twist_cos - part_imag * twist_sin]
    slice x12 -> x0, local copies, waits for them, and re-layouts: 76.1 us -> none  [the longest x5 23.2 us: shards(): layer_real = wave_real[layer_index][None]]
    unnamed x43 -> x8, local copies, waits for them, and re-layouts: 71.9 us -> 4.65 us
  transfers between devices with their start and end apart: 5 -> 13, of which waited for: 5 -> 12; matrix products, arithmetic and copies ran while one was open for 10% -> 1% of each run, Pallas kernels for 0% -> 32%
where the time goes in v1:
time: 862 us; the launch traced here: 860 us
  waiting for transfers between devices  449 us (52%)
  Pallas kernels  356 us (41%)
  starting transfers between devices  35.6 us (4%)
  local copies, waits for them, and re-layouts  17.9 us (2%)
    all_to_all x6, waiting for transfers between devices, exchange(): lax.all_to_all(values, ('row', 'col'), split_axis=0, concat_axis=0, tiled...  423 us
    pallas_call x4, Pallas kernels, row_inverse(): pl.pallas_call(row_inverse_kernel, grid_spec=pltpu.PrefetchScalarGridSpec...  102 us
    pallas_call x3, Pallas kernels, column_inverse(): pl.pallas_call(column_inverse_kernel, grid=(count, RADIX), in_specs=[pl.B...  84 us
    pallas_call x3, Pallas kernels, row_forward(): pl.pallas_call(row_forward_kernel, grid_spec=pltpu.PrefetchScalarGridSpec...  64.3 us
    pallas_call x3, Pallas kernels, column_forward(): pl.pallas_call(column_forward_kernel, grid=(count,), in_specs=[pl.BlockSp...  58.3 us
    pallas_call x1, Pallas kernels, partial_mix(): pl.pallas_call(partial_mix_kernel, grid=(RADIX, components), in_specs=[wa...  47.8 us
    all_to_all x6, starting transfers between devices, exchange(): lax.all_to_all(values, ('row', 'col'), split_axis=0, concat_axis=0, tiled...  32.1 us
    ppermute x7, waiting for transfers between devices, swap_cores(): return lax.ppermute(values, 'col', [(0, 1), (1, 0)])  25.8 us
  transfers between devices with their start and end apart: 13, of which 12 were waited for; matrix products, arithmetic and copies ran while one was open for 1% of the time, Pallas kernels for 32%

profile of v1, /device:TPU:17, one launch (start us, length us, event | category | flops | bytes accessed | tf_op | source)
XLA Modules:
  0.0 859.6 jit_solution(292624567638682066)
XLA Ops:
  0.0 3.2 constant_dynamic-slice_fusion.2
  4.7 3.2 collective-permute-done.other_ref
  9.2 16.8 %row_forward.3 = f32[16,1,2,128,256]{4,3,2,1,0:T(8,128)} custom-call(s32[1]{0:T(128)} %bitcast.core_ref, f32[4,512,2048]{2,1,0:T(8,128)} %own_ref.5, f32[1,256,2048]{2,1,0:T(8,128)} %copy-done.2, f32[16,2,8,256]{3,2,1,0:T(8,128)} %broadcast_multiply_fusion.twist_ref, bf16[2,256,256]{2,1,0:T(8,128)(2,1)} %constant.55.clone.table_ref), custom_call_target="tpu_custom_call" | custom-call | tf_op jit(solution)/shard_map/row_forward/pallas_call | solution.py:353
  26.0 6.2 all-to-all-start
  35.1 6.8 collective-permute-done.1.other_ref
  43.9 30.6 %row_forward.4 = f32[16,2,2,128,256]{4,3,2,1,0:T(8,128)} custom-call(s32[1]{0:T(128)} %bitcast.core_ref, f32[4,512,2048]{2,1,0:T(8,128)} %own_ref.5, f32[2,256,2048]{2,1,0:T(8,128)} %copy-done.1, f32[16,2,8,256]{3,2,1,0:T(8,128)} %broadcast_multiply_fusion.twist_ref, bf16[2,256,256]{2,1,0:T(8,128)(2,1)} %constant.55.clone.table_ref), custom_call_target="tpu_custom_call" | custom-call | tf_op jit(solution)/shard_map/row_forward/pallas_call | solution.py:353
  74.5 49.8 %all-to-all-done.x_ref = f32[16,1,2,128,256]{4,3,2,1,0:T(8,128)} async-done(((f32[16,1,2,128,256]{4,3,2,1,0:T(8,128)}), f32[16,1,2,128,256]{4,3,2,1,0:T(8,128)}, u32[]{:S(2)}, u32[]{:S(2)}) %all-to-all-start) | async-done | bytes 4194336 | tf_op jit(solution)/shard_map/all_to_all | solution.py:624
  124.3 5.2 all-to-all-start.1
  131.7 3.8 collective-permute-done.2.other_ref
  136.8 16.8 %row_forward.5 = f32[16,1,2,128,256]{4,3,2,1,0:T(8,128)} custom-call(s32[1]{0:T(128)} %bitcast.core_ref, f32[4,512,2048]{2,1,0:T(8,128)} %own_ref.5, f32[1,256,2048]{2,1,0:T(8,128)} %copy-done.3, f32[16,2,8,256]{3,2,1,0:T(8,128)} %broadcast_multiply_fusion.twist_ref, bf16[2,256,256]{2,1,0:T(8,128)(2,1)} %constant.55.clone.table_ref), custom_call_target="tpu_custom_call" | custom-call | tf_op jit(solution)/shard_map/row_forward/pallas_call | solution.py:353
  153.7 157.9 %all-to-all-done.1.x_ref = f32[16,2,2,128,256]{4,3,2,1,0:T(8,128)} async-done(((f32[16,2,2,128,256]{4,3,2,1,0:T(8,128)}), f32[16,2,2,128,256]{4,3,2,1,0:T(8,128)}, u32[]{:S(2)}, u32[]{:S(2)}) %all-to-all-start.1) | async-done | bytes 8388640 | tf_op jit(solution)/shard_map/all_to_all | solution.py:624
  311.6 5.2 all-to-all-start.2
  316.8 15.7 %column_forward.3.w0_ref = f32[1,2,128,4096]{3,2,1,0:T(8,128)} custom-call(f32[16,1,2,128,256]{4,3,2,1,0:T(8,128)} %all-to-all-done.x_ref, f32[16,2,8,256]{3,2,1,0:T(8,128)} %constant.54.clone.twist_ref, bf16[2,512,256]{2,1,0:T(8,128)(2,1)} %constant.56.clone.table_ref), custom_call_target="tpu_custom_call" | custom-call | tf_op jit(solution)/shard_map/column_forward/pallas_call | solution.py:382
  332.5 27.0 %column_forward.4.w1_ref.w2_ref = f32[2,2,128,4096]{3,2,1,0:T(8,128)} custom-call(f32[16,2,2,128,256]{4,3,2,1,0:T(8,128)} %all-to-all-done.1.x_ref, f32[16,2,8,256]{3,2,1,0:T(8,128)} %constant.54.clone.twist_ref, bf16[2,512,256]{2,1,0:T(8,128)(2,1)} %constant.56.clone.table_ref), custom_call_target="tpu_custom_call" | custom-call | tf_op jit(solution)/shard_map/column_forward/pallas_call | solution.py:382
  359.5 47.8 %partial_mix.1.sum_ref = f32[4,2,128,4096]{3,2,1,0:T(8,128)} custom-call(f32[1,2,128,4096]{3,2,1,0:T(8,128)} %column_forward.3.w0_ref, f32[2,2,128,4096]{3,2,1,0:T(8,128)} %column_forward.4.w1_ref.w2_ref, f32[2,2,128,4096]{3,2,1,0:T(8,128)} %column_forward.4.w1_ref.w2_ref, bf16[2,4,4,128,4096]{4,3,2,1,0:T(8,128)(2,1)} %unmix_ref.7), custom_call_target="tpu_custom_call" | custom-call | tf_op jit(solution)/shard_map/partial_mix/pallas_call | solution.py:409
  409.0 15.7 %column_forward.5.wave_ref = f32[1,2,128,4096]{3,2,1,0:T(8,128)} custom-call(f32[16,1,2,128,256]{4,3,2,1,0:T(8,128)} %all-to-all-done.2.x_ref, f32[16,2,8,256]{3,2,1,0:T(8,128)} %constant.54.clone.twist_ref, bf16[2,512,256]{2,1,0:T(8,128)(2,1)} %constant.56.clone.table_ref), custom_call_target="tpu_custom_call" | custom-call | tf_op jit(solution)/shard_map/column_forward/pallas_call | solution.py:382
  424.7 21.3 %column_inverse.5 = f32[16,1,2,256,128]{4,3,2,1,0:T(8,128)} custom-call(f32[4,2,128,4096]{3,2,1,0:T(8,128)} %partial_mix.1.sum_ref, f32[1,2,128,4096]{3,2,1,0:T(8,128)} %column_forward.5.wave_ref, bf16[2,4,4,128,4096]{4,3,2,1,0:T(8,128)(2,1)} %unmix_ref.7, f32[16,2,8,256]{3,2,1,0:T(8,128)} %constant.57.clone.twist_ref, ...), custom_call_target="tpu_custom_call" | custom-call | tf_op jit(solution)/shard_map/column_inverse/pallas_call | solution.py:427
  445.9 5.2 all-to-all-start.3
  451.1 41.4 %column_inverse.4 = f32[16,2,2,256,128]{4,3,2,1,0:T(8,128)} custom-call(f32[4,2,128,4096]{3,2,1,0:T(8,128)} %partial_mix.1.sum_ref, f32[1,2,128,4096]{3,2,1,0:T(8,128)} %column_forward.5.wave_ref, bf16[2,4,4,128,4096]{4,3,2,1,0:T(8,128)(2,1)} %unmix_ref.7, f32[16,2,8,256]{3,2,1,0:T(8,128)} %constant.57.clone.twist_ref, ...), custom_call_target="tpu_custom_call" | custom-call | tf_op jit(solution)/shard_map/column_inverse/pallas_call | solution.py:427
  492.5 50.8 %all-to-all-done.3.x_ref = f32[16,1,2,256,128]{4,3,2,1,0:T(8,128)} async-done(((f32[16,1,2,256,128]{4,3,2,1,0:T(8,128)}), f32[16,1,2,256,128]{4,3,2,1,0:T(8,128)}, u32[]{:S(2)}, u32[]{:S(2)}) %all-to-all-start.3) | async-done | bytes 4194336 | tf_op jit(solution)/shard_map/all_to_all | solution.py:624
  543.3 5.2 all-to-all-start.4
  548.5 25.5 %row_inverse.4 = (f32[4,512,2048]{2,1,0:T(8,128)}, f32[256,2048]{1,0:T(8,128)}) custom-call(s32[1]{0:T(128)} %bitcast.core_ref, f32[16,1,2,256,128]{4,3,2,1,0:T(8,128)} %all-to-all-done.3.x_ref, f32[32,2,8,128]{3,2,1,0:T(8,128)} %constant.59.clone.twist_ref, bf16[2,128,256]{2,1,0:T(8,128)(2,1)} %constant.60.clone.table_ref), custom_call_target="tpu_custom_call" | custom-call | tf_op jit(solution)/shard_map/row_inverse/pallas_call | solution.py:457
  574.3 21.3 %column_inverse.3 = f32[16,1,2,256,128]{4,3,2,1,0:T(8,128)} custom-call(f32[4,2,128,4096]{3,2,1,0:T(8,128)} %partial_mix.1.sum_ref, f32[1,2,128,4096]{3,2,1,0:T(8,128)} %column_forward.5.wave_ref, bf16[2,4,4,128,4096]{4,3,2,1,0:T(8,128)(2,1)} %unmix_ref.7, f32[16,2,8,256]{3,2,1,0:T(8,128)} %constant.57.clone.twist_ref, ...), custom_call_target="tpu_custom_call" | custom-call | tf_op jit(solution)/shard_map/column_inverse/pallas_call | solution.py:427
  595.7 134.9 %all-to-all-done.4.x_ref = f32[16,2,2,256,128]{4,3,2,1,0:T(8,128)} async-done(((f32[16,2,2,256,128]{4,3,2,1,0:T(8,128)}), f32[16,2,2,256,128]{4,3,2,1,0:T(8,128)}, u32[]{:S(2)}, u32[]{:S(2)}) %all-to-all-start.4) | async-done | bytes 8388640 | tf_op jit(solution)/shard_map/all_to_all | solution.py:624
  730.6 5.2 all-to-all-start.5
  737.2 25.4 %row_inverse.5 = (f32[4,512,2048]{2,1,0:T(8,128)}, f32[256,2048]{1,0:T(8,128)}) custom-call(s32[1]{0:T(128)} %bitcast.core_ref, f32[16,2,2,256,128]{4,3,2,1,0:T(8,128)} %all-to-all-done.4.x_ref, f32[32,2,8,128]{3,2,1,0:T(8,128)} %constant.59.clone.twist_ref, bf16[2,128,256]{2,1,0:T(8,128)(2,1)} %constant.60.clone.table_ref, ...), custom_call_target="tpu_custom_call", output_to_operand_aliasing={{0}: (4, {})} | custom-call | tf_op jit(solution)/shard_map/row_inverse/pallas_call | solution.py:457
  763.0 4.0 collective-permute-done.4
  768.5 25.4 %row_inverse.6 = (f32[4,512,2048]{2,1,0:T(8,128)}, f32[256,2048]{1,0:T(8,128)}) custom-call(s32[1]{0:T(128)} %bitcast.core_ref, f32[16,2,2,256,128]{4,3,2,1,0:T(8,128)} %all-to-all-done.4.x_ref, f32[32,2,8,128]{3,2,1,0:T(8,128)} %constant.59.clone.twist_ref, bf16[2,128,256]{2,1,0:T(8,128)(2,1)} %constant.60.clone.table_ref, ...), custom_call_target="tpu_custom_call", output_to_operand_aliasing={{0}: (4, {})} | custom-call | tf_op jit(solution)/shard_map/row_inverse/pallas_call | solution.py:457
  794.2 4.0 collective-permute-done.5
  799.7 28.3 %all-to-all-done.5.x_ref = f32[16,1,2,256,128]{4,3,2,1,0:T(8,128)} async-done(((f32[16,1,2,256,128]{4,3,2,1,0:T(8,128)}), f32[16,1,2,256,128]{4,3,2,1,0:T(8,128)}, u32[]{:S(2)}, u32[]{:S(2)}) %all-to-all-start.5) | async-done | bytes 4194336 | tf_op jit(solution)/shard_map/all_to_all | solution.py:624
  827.9 25.4 %row_inverse.7 = (f32[4,512,2048]{2,1,0:T(8,128)}, f32[256,2048]{1,0:T(8,128)}) custom-call(s32[1]{0:T(128)} %bitcast.core_ref, f32[16,1,2,256,128]{4,3,2,1,0:T(8,128)} %all-to-all-done.5.x_ref, f32[32,2,8,128]{3,2,1,0:T(8,128)} %constant.59.clone.twist_ref, bf16[2,128,256]{2,1,0:T(8,128)(2,1)} %constant.60.clone.table_ref, ...), custom_call_target="tpu_custom_call", output_to_operand_aliasing={{0}: (4, {})} | custom-call | tf_op jit(solution)/shard_map/row_inverse/pallas_call | solution.py:457
  854.2 4.0 collective-permute-done.6
  (25 shorter events, 20.7 us)
Async XLA Ops:
  0.0 3.9 copy-start
  3.2 4.7 collective-permute-start
  7.9 1.3 copy-start.2
  26.0 98.4 %all-to-all-start = ((f32[16,1,2,128,256]{4,3,2,1,0:T(8,128)}), f32[16,1,2,128,256]{4,3,2,1,0:T(8,128)}, u32[]{:S(2)}, u32[]{:S(2)}) async-start(f32[16,1,2,128,256]{4,3,2,1,0:T(8,128)} %row_forward.3), calls=%async_computation | async-start | bytes 8388608 | tf_op jit(solution)/shard_map/all_to_all | solution.py:624
  34.6 7.2 collective-permute-start.1
  41.9 2.0 copy-start.1
  124.3 187.3 %all-to-all-start.1 = ((f32[16,2,2,128,256]{4,3,2,1,0:T(8,128)}), f32[16,2,2,128,256]{4,3,2,1,0:T(8,128)}, u32[]{:S(2)}, u32[]{:S(2)}) async-start(f32[16,2,2,128,256]{4,3,2,1,0:T(8,128)} %row_forward.4), calls=%async_computation.1 | async-start | bytes 16777216 | tf_op jit(solution)/shard_map/all_to_all | solution.py:624
  131.3 4.2 collective-permute-start.2
  135.5 1.3 copy-start.3
  311.6 97.4 %all-to-all-start.2 = ((f32[16,1,2,128,256]{4,3,2,1,0:T(8,128)}), f32[16,1,2,128,256]{4,3,2,1,0:T(8,128)}, u32[]{:S(2)}, u32[]{:S(2)}) async-start(f32[16,1,2,128,256]{4,3,2,1,0:T(8,128)} %row_forward.5), calls=%async_computation.2 | async-start | bytes 8388608 | tf_op jit(solution)/shard_map/all_to_all | solution.py:624
  445.9 97.4 %all-to-all-start.3 = ((f32[16,1,2,256,128]{4,3,2,1,0:T(8,128)}), f32[16,1,2,256,128]{4,3,2,1,0:T(8,128)}, u32[]{:S(2)}, u32[]{:S(2)}) async-start(f32[16,1,2,256,128]{4,3,2,1,0:T(8,128)} %column_inverse.5), calls=%async_computation.3 | async-start | bytes 8388608 | tf_op jit(solution)/shard_map/all_to_all | solution.py:624
  543.3 187.3 %all-to-all-start.4 = ((f32[16,2,2,256,128]{4,3,2,1,0:T(8,128)}), f32[16,2,2,256,128]{4,3,2,1,0:T(8,128)}, u32[]{:S(2)}, u32[]{:S(2)}) async-start(f32[16,2,2,256,128]{4,3,2,1,0:T(8,128)} %column_inverse.4), calls=%async_computation.4 | async-start | bytes 16777216 | tf_op jit(solution)/shard_map/all_to_all | solution.py:624
  574.0 161.8 %collective-permute-start.3 = (f32[256,2048]{1,0:T(8,128)}, f32[256,2048]{1,0:T(8,128)S(1)}, u32[]{:S(2)}, u32[]{:S(2)}) collective-permute-start(f32[256,2048]{1,0:T(8,128)} %get-tuple-element.32), channel_id=1, source_target_pairs={{0,1},{1,0},{2,3},{3,2},{4,5},{5,4},{6,7},{7,6},{8,9},{9,8},{10,11... | collective-permute-start | bytes 6291464 | tf_op jit(solution)/shard_map/ppermute | solution.py:620
  730.6 97.4 %all-to-all-start.5 = ((f32[16,1,2,256,128]{4,3,2,1,0:T(8,128)}), f32[16,1,2,256,128]{4,3,2,1,0:T(8,128)}, u32[]{:S(2)}, u32[]{:S(2)}) async-start(f32[16,1,2,256,128]{4,3,2,1,0:T(8,128)} %column_inverse.3), calls=%async_computation.5 | async-start | bytes 8388608 | tf_op jit(solution)/shard_map/all_to_all | solution.py:624
  762.6 4.4 collective-permute-start.4
  793.8 4.4 collective-permute-start.5
  853.3 4.9 collective-permute-start.6

commit v2 on v1

--- a/solution.py
+++ b/solution.py
@@ -1,3 +1,4 @@
+import functools
 import math
 
 import jax
@@ -10,6 +11,7 @@
 from jax.sharding import PartitionSpec as P
 
 RADIX = 16
+PACKED = 64
 
 
 def split_table(table):
@@ -136,7 +138,14 @@
     return real, imag
 
 
-def row_forward_kernel(core_ref, own_ref, other_ref, twist_ref, table_ref, out_ref, part_ref):
+def combine_packed(products, out_len):
+    swapped = pltpu.roll(products[out_len:], PACKED, 1)
+    lane = lax.broadcasted_iota(jnp.int32, swapped.shape, 1)
+    return products[:out_len] + jnp.where(lane < PACKED, -swapped, swapped)
+
+
+def row_forward_kernel(core_ref, own_ref, other_ref, twist_ref, table_ref, *refs):
+    *out_refs, part_ref = refs
     rows = own_ref.shape[1]
     width = part_ref.shape[2]
     per_half = RADIX // 2
@@ -157,16 +166,19 @@
         return 0
 
     lax.fori_loop(0, rows // 8, small, 0)
-    blocks, _, _, per_block, _ = out_ref.shape
-    out_len = blocks * per_block // RADIX
-    piece = per_block // RADIX
+    blocks, _, _, per_part, _ = out_refs[0].shape
+    piece = per_part // RADIX
+    per_block = piece * len(out_refs)
 
     def line(index, _):
-        real, imag = combine(matmul_split(table_ref, part_ref[index]), out_len, rows)
+        values = combine(matmul_split(table_ref, part_ref[index]), blocks * per_block, rows)
         for block in range(blocks):
-            place = pl.ds(index, piece, stride=RADIX)
-            out_ref[block, 0, 0, place, :] = real[block * piece : (block + 1) * piece]
-            out_ref[block, 0, 1, place, :] = imag[block * piece : (block + 1) * piece]
+            for part, out_ref in enumerate(out_refs):
+                start = block * per_block + part * piece
+                for side, value in enumerate(values):
+                    out_ref[block, 0, side, pl.ds(index, piece, stride=RADIX), :] = value[
+                        start : start + piece
+                    ]
         return 0
 
     lax.fori_loop(0, RADIX, line, 0)
@@ -200,62 +212,43 @@
     complex_lines(read, rows, width, -1, twist_ref, part_ref)
 
     def line(index, _):
-        real, imag = combine(matmul_split(table_ref, part_ref[index]), width, rows)
-        order_ref[0, pl.ds(index, width, stride=RADIX), :] = real
-        order_ref[1, pl.ds(index, width, stride=RADIX), :] = imag
+        order_ref[pl.ds(index, width, stride=RADIX), :] = combine_packed(
+            matmul_split(table_ref, part_ref[index]), width
+        )
         return 0
 
     lax.fori_loop(0, RADIX, line, 0)
 
     def flip(index, _):
         start = pl.multiple_of(index * width, width)
-        for part in range(2):
-            out_ref[0, part, :, pl.ds(start, width)] = order_ref[part, pl.ds(start, width), :].T
+        flipped = order_ref[pl.ds(start, width), :].T
+        out_ref[0, 0, :, pl.ds(start, width)] = flipped[:rows]
+        out_ref[0, 1, :, pl.ds(start, width)] = flipped[rows:]
         return 0
 
     lax.fori_loop(0, RADIX, flip, 0)
 
 
-def mix_rows(waves, unmix_ref, row, real, imag):
-    for layer, wave in enumerate(waves):
-        weight_real = unmix_ref[0, 0, layer, pl.ds(row, 16), :].astype(jnp.float32)
-        weight_imag = unmix_ref[1, 0, layer, pl.ds(row, 16), :].astype(jnp.float32)
-        wave_real = wave[0, 0, pl.ds(row, 16), :]
-        wave_imag = wave[0, 1, pl.ds(row, 16), :]
-        term_real = weight_real * wave_real - weight_imag * wave_imag
-        term_imag = weight_real * wave_imag + weight_imag * wave_real
-        real = term_real if real is None else real + term_real
-        imag = term_imag if imag is None else imag + term_imag
-    return real, imag
-
-
-def partial_mix_kernel(w0_ref, w1_ref, w2_ref, unmix_ref, out_ref):
-    def mix(block, _):
-        row = pl.multiple_of(block * 16, 16)
-        real, imag = mix_rows((w0_ref, w1_ref, w2_ref), unmix_ref, row, None, None)
-        out_ref[0, 0, pl.ds(row, 16), :] = real
-        out_ref[0, 1, pl.ds(row, 16), :] = imag
-        return 0
-
-    lax.fori_loop(0, out_ref.shape[2] // 16, mix, 0)
-
-
 def column_inverse_kernel(
-    sum_ref, wave_ref, unmix_ref, twist_ref, table_ref, out_ref, mixed_ref, part_ref
+    counts, w0_ref, w1_ref, w2_ref, w3_ref, unmix_ref, twist_ref, table_ref, *refs
 ):
+    *out_refs, mixed_ref, part_ref = refs
+    component = pl.program_id(0)
     step = pl.program_id(1)
     rows = mixed_ref.shape[2]
     width = mixed_ref.shape[3]
 
     def mix(block, _):
         row = pl.multiple_of(block * 16, 16)
-        real, imag = mix_rows(
-            (wave_ref,),
-            unmix_ref,
-            row,
-            sum_ref[0, 0, pl.ds(row, 16), :],
-            sum_ref[0, 1, pl.ds(row, 16), :],
-        )
+        for layer, wave in enumerate((w0_ref, w1_ref, w2_ref, w3_ref)):
+            weight_real = unmix_ref[0, 0, layer, pl.ds(row, 16), :].astype(jnp.float32)
+            weight_imag = unmix_ref[1, 0, layer, pl.ds(row, 16), :].astype(jnp.float32)
+            wave_real = wave[0, 0, pl.ds(row, 16), :]
+            wave_imag = wave[0, 1, pl.ds(row, 16), :]
+            term_real = weight_real * wave_real - weight_imag * wave_imag
+            term_imag = weight_real * wave_imag + weight_imag * wave_real
+            real = term_real if layer == 0 else real + term_real
+            imag = term_imag if layer == 0 else imag + term_imag
         mixed_ref[step, 0, pl.ds(row, 16), :] = real
         mixed_ref[step, 1, pl.ds(row, 16), :] = imag
         return 0
@@ -268,34 +261,50 @@
             return mixed_ref[index, part, row, lanes]
 
         complex_lines(read, rows, width, 1, twist_ref, part_ref)
-        blocks, _, _, per_block, _ = out_ref.shape
+        blocks, _, per_block, _ = out_refs[0].shape
         piece = per_block // RADIX
 
-        def line(index, _):
-            real, imag = combine(matmul_split(table_ref, part_ref[index]), width, rows)
-            for block in range(blocks):
-                place = pl.ds(index, piece, stride=RADIX)
-                out_ref[block, 0, 0, place, :] = real[block * piece : (block + 1) * piece]
-                out_ref[block, 0, 1, place, :] = imag[block * piece : (block + 1) * piece]
-            return 0
-
-        lax.fori_loop(0, RADIX, line, 0)
-
-
-def row_inverse_kernel(core_ref, x_ref, twist_ref, table_ref, *refs):
+        def lines(out_ref):
+            def line(index, _):
+                packed = combine_packed(matmul_split(table_ref, part_ref[index]), width)
+                for block in range(blocks):
+                    out_ref[block, 0, pl.ds(index, piece, stride=RADIX), :] = packed[
+                        block * piece : (block + 1) * piece
+                    ]
+                return 0
+
+            lax.fori_loop(0, RADIX, line, 0)
+
+        first = 0
+        for count, out_ref in zip(counts, out_refs):
+            inside = (component >= first) & (component < first + count)
+            pl.when(inside)(functools.partial(lines, out_ref))
+            first += count
+
+
+def row_inverse_kernel(core_ref, low_ref, high_ref, twist_ref, table_ref, *refs):
     out_ref, sent_ref, part_ref, order_ref = refs[-4:]
-    rows = x_ref.shape[3]
-    width = x_ref.shape[4]
+    rows = low_ref.shape[2]
+    width = low_ref.shape[3]
     count = 2 * RADIX
     lanes = pl.ds(0, width)
+    first_lanes = lax.broadcasted_iota(jnp.int32, (8, width), 1) < PACKED
 
     def small(step, _):
         row = pl.multiple_of(step * 8, 8)
+        packed = [
+            (low_ref[index, 0, pl.ds(row, 8), :], high_ref[index, 0, pl.ds(row, 8), :])
+            for index in range(RADIX)
+        ]
+        whole_values = [
+            (
+                jnp.where(first_lanes, low, pltpu.roll(high, PACKED, 1)),
+                jnp.where(first_lanes, pltpu.roll(low, PACKED, 1), high),
+            )
+            for low, high in packed
+        ]
         for odd in range(2):
-            values = [
-                (x_ref[index, 0, 0, pl.ds(row, 8), :], x_ref[index, 0, 1, pl.ds(row, 8), :])
-                for index in range(RADIX)
-            ]
+            values = whole_values
             if odd:
                 values = [turn(value, index, count) for index, value in enumerate(values)]
             for index, value in enumerate(small_fourier(values, 1)):
@@ -312,7 +321,7 @@
         return 0
 
     lax.fori_loop(0, count, line, 0)
-    half_len = sent_ref.shape[1]
+    half_len = sent_ref.shape[2]
     chunk = 256
     own = core_ref[0] * half_len
     other = half_len - own
@@ -321,7 +330,7 @@
         start = pl.multiple_of(index * chunk, chunk)
         own_start = pl.multiple_of(own + start, chunk)
         other_start = pl.multiple_of(other + start, chunk)
-        sent_ref[:, pl.ds(start, chunk)] = order_ref[pl.ds(other_start, chunk), :].T
+        sent_ref[0, :, pl.ds(start, chunk)] = order_ref[pl.ds(other_start, chunk), :].T
         out_ref[0, :, pl.ds(start, chunk)] = order_ref[pl.ds(own_start, chunk), :].T
         return 0
 
@@ -342,11 +351,12 @@
     )
 
 
-def row_forward(layers, other, core, first, blocks, per_block):
+def row_forward(layers, other, core, first, blocks, per_block, parts):
     count, rows, half_len = other.shape
     length = 2 * half_len
     width = length // RADIX
     tiles = rows // ROW_TILE
+    per_part = per_block // parts
     signs = jnp.where(jnp.arange(RADIX) % 2 == 1, 1.0 - 2.0 * core[0].astype(jnp.float32), 1.0)
     twists = jnp.asarray(twiddle_table(RADIX, width, length, -1)) * signs[:, None, None, None]
     table = jnp.asarray(line_table(blocks * per_block // RADIX, width, -1))
@@ -363,12 +373,13 @@
                 whole(twists),
                 whole(table),
             ],
-            out_specs=pl.BlockSpec(
-                (blocks, 1, 2, per_block, ROW_TILE), lambda m, i, c: (0, m, 0, 0, i)
-            ),
+            out_specs=[
+                pl.BlockSpec((blocks, 1, 2, per_part, ROW_TILE), lambda m, i, c: (0, m, 0, 0, i))
+            ]
+            * parts,
             scratch_shapes=[pltpu.VMEM((RADIX, 2 * ROW_TILE, width), jnp.float32)],
         ),
-        out_shape=jax.ShapeDtypeStruct((blocks, count, 2, per_block, rows), jnp.float32),
+        out_shape=[jax.ShapeDtypeStruct((blocks, count, 2, per_part, rows), jnp.float32)] * parts,
         compiler_params=params(2),
         name="row_forward",
     )(core, layers, other, twists, table)
@@ -381,72 +392,64 @@
     table = jnp.asarray(line_table(width, width, -1))
     return pl.pallas_call(
         column_forward_kernel,
-        grid=(count,),
+        grid=(count, rows // PACKED),
         in_specs=[
-            pl.BlockSpec((blocks, 1, 2, rows, width), lambda m: (0, m, 0, 0, 0)),
+            pl.BlockSpec((blocks, 1, 2, PACKED, width), lambda m, i: (0, m, 0, i, 0)),
             whole(twists),
             whole(table),
         ],
-        out_specs=pl.BlockSpec((1, 2, rows, length), lambda m: (m, 0, 0, 0)),
+        out_specs=pl.BlockSpec((1, 2, PACKED, length), lambda m, i: (m, 0, i, 0)),
         out_shape=jax.ShapeDtypeStruct((count, 2, rows, length), jnp.float32),
         scratch_shapes=[
-            pltpu.VMEM((RADIX, 2 * rows, width), jnp.float32),
-            pltpu.VMEM((2, length, rows), jnp.float32),
+            pltpu.VMEM((RADIX, 2 * PACKED, width), jnp.float32),
+            pltpu.VMEM((length, 2 * PACKED), jnp.float32),
         ],
-        compiler_params=params(1),
+        compiler_params=params(2),
         name="column_forward",
     )(x, twists, table)
 
 
-def partial_mix(waves, unmixing):
-    components = unmixing.shape[1]
-    _, _, rows, length = waves[0][0].shape
-    width = length // RADIX
-
-    def wave_spec(place):
-        return pl.BlockSpec((1, 2, rows, width), lambda i, j: (place, 0, 0, i))
-
-    return pl.pallas_call(
-        partial_mix_kernel,
-        grid=(RADIX, components),
-        in_specs=[wave_spec(place) for _, place in waves]
-        + [pl.BlockSpec((2, 1, len(waves), rows, width), lambda i, j: (0, j, 0, 0, i))],
-        out_specs=pl.BlockSpec((1, 2, rows, width), lambda i, j: (j, 0, 0, i)),
-        out_shape=jax.ShapeDtypeStruct((components, 2, rows, length), jnp.float32),
-        compiler_params=params(2),
-        name="partial_mix",
-    )(*[wave for wave, _ in waves], unmixing)
-
-
-def column_inverse(sums, wave, place, layer, unmixing, first, count, blocks):
-    _, _, rows, length = sums.shape
+def column_inverse(waves, unmixing, half, counts, blocks):
+    length = waves[0][0].shape[3]
     width = length // RADIX
     per_block = length // blocks
     twists = jnp.asarray(twiddle_table(RADIX, width, length, 1))
     table = jnp.asarray(line_table(width, width, 1))
+
+    def wave_spec(place, part):
+        return pl.BlockSpec((1, 2, PACKED, width), lambda j, i: (place, 0, part, i))
+
+    def out_spec(first, count):
+        return pl.BlockSpec(
+            (blocks, 1, per_block, 2 * PACKED),
+            lambda j, i: (0, jnp.clip(j - first, 0, count - 1), 0, 0),
+        )
+
     return pl.pallas_call(
-        column_inverse_kernel,
-        grid=(count, RADIX),
-        in_specs=[
-            pl.BlockSpec((1, 2, rows, width), lambda j, i: (first + j, 0, 0, i)),
-            pl.BlockSpec((1, 2, rows, width), lambda j, i: (place, 0, 0, i)),
-            pl.BlockSpec((2, 1, 1, rows, width), lambda j, i: (0, first + j, layer, 0, i)),
+        functools.partial(column_inverse_kernel, counts),
+        grid=(sum(counts), RADIX),
+        in_specs=[wave_spec(place, part) for _, place, part in waves]
+        + [
+            pl.BlockSpec((2, 1, len(waves), PACKED, width), lambda j, i: (0, j, 0, half, i)),
             whole(twists),
             whole(table),
         ],
-        out_specs=pl.BlockSpec((blocks, 1, 2, per_block, rows), lambda j, i: (0, j, 0, 0, 0)),
-        out_shape=jax.ShapeDtypeStruct((blocks, count, 2, per_block, rows), jnp.float32),
+        out_specs=[out_spec(sum(counts[:place]), count) for place, count in enumerate(counts)],
+        out_shape=[
+            jax.ShapeDtypeStruct((blocks, count, per_block, 2 * PACKED), jnp.float32)
+            for count in counts
+        ],
         scratch_shapes=[
-            pltpu.VMEM((RADIX, 2, rows, width), jnp.float32),
-            pltpu.VMEM((RADIX, 2 * rows, width), jnp.float32),
+            pltpu.VMEM((RADIX, 2, PACKED, width), jnp.float32),
+            pltpu.VMEM((RADIX, 2 * PACKED, width), jnp.float32),
         ],
         compiler_params=params(2),
         name="column_inverse",
-    )(sums, wave, unmixing, twists, table)
-
-
-def row_inverse(x, place, component, shape, fields, core, scale):
-    blocks, _, _, rows, width = x.shape
+    )(*[wave for wave, _, _ in waves], unmixing, twists, table)
+
+
+def row_inverse(low, high, first, group, shape, fields, core, scale):
+    blocks, _, rows, width = low[0].shape
     half_len = shape[2]
     length = 2 * half_len
     count = 2 * RADIX
@@ -454,22 +457,22 @@
     twists = jnp.asarray(twiddle_table(count, width, length, 1))
     table = jnp.asarray(real_table(length // count, width, scale))
     held = [] if fields is None else [fields]
+
+    def packed_spec(place):
+        return pl.BlockSpec((blocks, 1, ROW_TILE, width), lambda m, i, c: (0, place + m, i, 0))
+
     return pl.pallas_call(
         row_inverse_kernel,
         grid_spec=pltpu.PrefetchScalarGridSpec(
             num_scalar_prefetch=1,
-            grid=(tiles,),
-            in_specs=[
-                pl.BlockSpec((blocks, 1, 2, ROW_TILE, width), lambda i, c: (0, place, 0, i, 0)),
-                whole(twists),
-                whole(table),
-            ]
+            grid=(group, tiles),
+            in_specs=[packed_spec(low[1]), packed_spec(high[1]), whole(twists), whole(table)]
             + [pl.BlockSpec(memory_space=pl.ANY)] * len(held),
             out_specs=[
                 pl.BlockSpec(
-                    (1, ROW_TILE, half_len), lambda i, c: (component, c[0] * tiles + i, 0)
+                    (1, ROW_TILE, half_len), lambda m, i, c: (first + m, c[0] * tiles + i, 0)
                 ),
-                pl.BlockSpec((ROW_TILE, half_len), lambda i, c: (i, 0)),
+                pl.BlockSpec((1, ROW_TILE, half_len), lambda m, i, c: (m, i, 0)),
             ],
             scratch_shapes=[
                 pltpu.VMEM((count, ROW_TILE, 2 * width), jnp.float32),
@@ -478,12 +481,12 @@
         ),
         out_shape=[
             jax.ShapeDtypeStruct(shape, jnp.float32),
-            jax.ShapeDtypeStruct((rows, half_len), jnp.float32),
+            jax.ShapeDtypeStruct((group, rows, half_len), jnp.float32),
         ],
-        input_output_aliases={4: 0} if held else {},
-        compiler_params=params(1),
+        input_output_aliases={5: 0} if held else {},
+        compiler_params=params(2),
         name="row_inverse",
-    )(core, x, twists, table, *held)
+    )(core, low[0], high[0], twists, table, *held)
 
 
 def phase_pair(first_len, second_len, period, sign):
@@ -620,51 +623,59 @@
     return lax.ppermute(values, "col", [(0, 1), (1, 0)])
 
 
-def exchange(values):
-    return lax.all_to_all(values, ("row", "col"), split_axis=0, concat_axis=0, tiled=True)
+def exchange_all(ready):
+    moved = []
+    for values in ready:
+        if moved:
+            values, moved[-1] = lax.optimization_barrier((values, moved[-1]))
+        moved.append(
+            lax.all_to_all(values, ("row", "col"), split_axis=0, concat_axis=0, tiled=True)
+        )
+    return moved
 
 
 def layer_shards(layers, unmixing):
     row_count = lax.axis_size("row")
     col_count = lax.axis_size("col")
     blocks = row_count * col_count
-    _, block_rows, half_len = layers.shape
+    layer_count, block_rows, half_len = layers.shape
     rows = block_rows // col_count
     per_block = unmixing.shape[3]
     core = lax.axis_index("col").astype(jnp.int32).reshape(1)
-    own_row = core[0] * rows
-    other_row = rows - own_row
-    groups = ((0, 1), (1, 2), (3, 1))
-
-    source = layers
-    moved = None
-    arrived = []
-    for first, count in groups:
+    other_row = rows - core[0] * rows
+
+    def lines(source, first, count, parts):
         given = lax.dynamic_slice(source, (first, other_row, 0), (count, rows, half_len))
-        spectra = row_forward(layers, swap_cores(given), core, first, blocks, per_block)
-        source, spectra = lax.optimization_barrier((source, spectra))
-        if moved is not None:
-            spectra, moved = lax.optimization_barrier((spectra, moved))
-        moved = exchange(spectra)
-        arrived.append(moved)
+        other = swap_cores(given)
+        return row_forward(layers, other, core, first, blocks, per_block, parts)
+
+    (head,) = lines(layers, 0, 1, 1)
+    source, head = lax.optimization_barrier((layers, head))
+    rest = lines(source, 1, layer_count - 1, 2)
+    first_moved, *rest_moved = exchange_all([head, *rest])
+    first_wave = column_forward(first_moved)
     waves = []
-    for (_, count), moved in zip(groups, arrived):
-        group = column_forward(moved)
-        waves += [(group, place) for place in range(count)]
-    sums = partial_mix(waves[:3], unmixing)
+    for half, moved in enumerate(rest_moved):
+        rest_waves = column_forward(moved)
+        waves.append(
+            [(first_wave, 0, half)] + [(rest_waves, place, 0) for place in range(layer_count - 1)]
+        )
+    early = unmixing.shape[1] - 1
+    low, low_last = column_inverse(waves[0], unmixing, 0, (early, 1), blocks)
+    high, high_last = column_inverse(waves[1], unmixing, 1, (early, 1), blocks)
+    low, *_ = lax.optimization_barrier((low, rest_moved[-1]))
+    last = jnp.concatenate([low_last, high_last], axis=1)
+    low, high, last = exchange_all([low, high, last])
     scale = 2.0 / (block_rows * row_count * half_len * col_count)
     fields = None
-    for first, count in groups:
-        back = column_inverse(sums, *waves[3], 3, unmixing, first, count, blocks)
-        if first > 0:
-            back, sent = lax.optimization_barrier((back, sent))
-        sent = exchange(back)
-        for place in range(count):
-            fields, given = row_inverse(
-                sent, place, first + place, layers.shape, fields, core, scale
-            )
-            taken = swap_cores(given)[None]
-            fields = lax.dynamic_update_slice(fields, taken, (first + place, other_row, 0))
+    for first, group, low_part, high_part in (
+        (0, early, (low, 0), (high, 0)),
+        (early, 1, (last, 0), (last, 1)),
+    ):
+        fields, given = row_inverse(
+            low_part, high_part, first, group, layers.shape, fields, core, scale
+        )
+        fields = lax.dynamic_update_slice(fields, swap_cores(given), (first, other_row, 0))
     return fields
 
 

time: 862 us -> 828 us (0.961)
  waiting for transfers between devices: 449 us -> 219 us
  blocking collectives: 0 us -> 142 us
  Pallas kernels: 356 us -> 414 us
    all_to_all x6 -> x5, waiting for transfers between devices: 423 us -> 193 us  [exchange_all(): lax.all_to_all(values, ('row', 'col'), split_axis=0, concat_axis=0, tiled...]
    all_to_all x0 -> x1, blocking collectives: none -> 142 us  [exchange_all(): lax.all_to_all(values, ('row', 'col'), split_axis=0, concat_axis=0, tiled...]
    pallas_call x7 -> x5, Pallas kernels: 190 us -> 246 us  [the longest x2 160 us: column_inverse(): pl.pallas_call(functools.partial(column_inverse_kernel, counts), grid=(su...]
    all_to_all x6 -> x5, starting transfers between devices: 32.1 us -> 27.6 us  [exchange_all(): lax.all_to_all(values, ('row', 'col'), split_axis=0, concat_axis=0, tiled...]
    pallas_call x4 -> x2, Pallas kernels: 102 us -> 106 us  [row_inverse(): pl.pallas_call(row_inverse_kernel, grid_spec=pltpu.PrefetchScalarGridSpec...]
    pallas_call x3 -> x2, Pallas kernels: 64.3 us -> 61.9 us  [row_forward(): pl.pallas_call(row_forward_kernel, grid_spec=pltpu.PrefetchScalarGridSpec...]
    ppermute x7 -> x4, waiting for transfers between devices: 25.8 us -> 26.1 us  [swap_cores(): return lax.ppermute(values, 'col', [(0, 1), (1, 0)])]
  transfers between devices with their start and end apart: 13 -> 9, of which waited for: 12 -> 9; matrix products, arithmetic and copies ran while one was open for 1% -> 1% of each run, Pallas kernels for 32% -> 45%
where the time goes in v2:
time: 828 us; the launch traced here: 826 us
  Pallas kernels  414 us (50%)
  waiting for transfers between devices  219 us (26%)
  blocking collectives  142 us (17%)
  starting transfers between devices  29.9 us (4%)
  local copies, waits for them, and re-layouts  15 us (2%)
    all_to_all x5, waiting for transfers between devices, exchange_all(): lax.all_to_all(values, ('row', 'col'), split_axis=0, concat_axis=0, tiled...  193 us
    pallas_call x2, Pallas kernels, column_inverse(): pl.pallas_call(functools.partial(column_inverse_kernel, counts), grid=(su...  160 us
    all_to_all x1, blocking collectives, exchange_all(): lax.all_to_all(values, ('row', 'col'), split_axis=0, concat_axis=0, tiled...  142 us
    pallas_call x2, Pallas kernels, row_inverse(): pl.pallas_call(row_inverse_kernel, grid_spec=pltpu.PrefetchScalarGridSpec...  106 us
    pallas_call x3, Pallas kernels, column_forward(): pl.pallas_call(column_forward_kernel, grid=(count, rows // PACKED), in_sp...  86.3 us
    pallas_call x2, Pallas kernels, row_forward(): pl.pallas_call(row_forward_kernel, grid_spec=pltpu.PrefetchScalarGridSpec...  61.9 us
    all_to_all x5, starting transfers between devices, exchange_all(): lax.all_to_all(values, ('row', 'col'), split_axis=0, concat_axis=0, tiled...  27.6 us
    ppermute x4, waiting for transfers between devices, swap_cores(): return lax.ppermute(values, 'col', [(0, 1), (1, 0)])  26.1 us
  transfers between devices with their start and end apart: 9, of which 9 were waited for; matrix products, arithmetic and copies ran while one was open for 1% of the time, Pallas kernels for 45%

profile of v2, /device:TPU:17, one launch (start us, length us, event | category | flops | bytes accessed | tf_op | source)
XLA Modules:
  0.0 825.7 jit_solution(8538313229417610208)
XLA Ops:
  0.0 3.1 constant_dynamic-slice_fusion.1
  3.8 1.7 broadcast_multiply_fusion.twist_ref
  5.6 2.3 collective-permute-done.other_ref
  7.8 1.3 copy-done.1
  9.1 16.8 %row_forward.2 = f32[16,1,2,128,256]{4,3,2,1,0:T(8,128)} custom-call(s32[1]{0:T(128)} %bitcast.core_ref, f32[4,512,2048]{2,1,0:T(8,128)} %own_ref.3, f32[1,256,2048]{2,1,0:T(8,128)} %copy-done.1, f32[16,2,8,256]{3,2,1,0:T(8,128)} %broadcast_multiply_fusion.twist_ref, bf16[2,256,256]{2,1,0:T(8,128)(2,1)} %constant.52.clone.table_ref), custom_call_target="tpu_custom_call" | custom-call | tf_op jit(solution)/shard_map/row_forward/pallas_call | solution.py:363
  25.9 6.2 all-to-all-start
  32.1 3.2 constant_dynamic-slice_fusion
  35.7 9.8 %collective-permute-done.1.other_ref = f32[3,256,2048]{2,1,0:T(8,128)S(1)} collective-permute-done((f32[3,256,2048]{2,1,0:T(8,128)S(1)}, f32[3,256,2048]{2,1,0:T(8,128)S(1)}, u32[]{:S(2)}, u32[]{:S(2)}) %collective-permute-start.1) | collective-permute-done | bytes 6291488 | tf_op jit(solution)/shard_map/ppermute | solution.py:623
  45.5 2.7 copy-done
  48.2 45.1 %row_forward.3 = (f32[16,3,2,64,256]{4,3,2,1,0:T(8,128)}, f32[16,3,2,64,256]{4,3,2,1,0:T(8,128)}) custom-call(s32[1]{0:T(128)} %bitcast.core_ref, f32[4,512,2048]{2,1,0:T(8,128)} %own_ref.3, f32[3,256,2048]{2,1,0:T(8,128)} %copy-done, f32[16,2,8,256]{3,2,1,0:T(8,128)} %broadcast_multiply_fusion.twist_ref, bf16[2,256,256]{2,1,0:T(8,128)(2,1)} %constant.52.clone.table_ref), custom_call_target="tpu_custom_call" | custom-call | tf_op jit(solution)/shard_map/row_forward/pallas_call | solution.py:363
  93.4 30.9 %all-to-all-done.x_ref = f32[16,1,2,128,256]{4,3,2,1,0:T(8,128)} async-done(((f32[16,1,2,128,256]{4,3,2,1,0:T(8,128)}), f32[16,1,2,128,256]{4,3,2,1,0:T(8,128)}, u32[]{:S(2)}, u32[]{:S(2)}) %all-to-all-start) | async-done | bytes 4194336 | tf_op jit(solution)/shard_map/all_to_all | solution.py:632
  124.3 142.2 %all_to_all.30.x_ref = f32[16,3,2,64,256]{4,3,2,1,0:T(8,128)} all-to-all(f32[16,3,2,64,256]{4,3,2,1,0:T(8,128)} %get-tuple-element.31), channel_id=1, replica_groups=mesh['tiles'=2,'row'=8,'col'=2] {'row','col'}, dimensions={0} | all-to-all | bytes 12582912 | tf_op jit(solution)/shard_map/all_to_all | solution.py:632
  266.5 5.7 all-to-all-start.2
  272.3 22.3 %column_forward.3.w0_ref = f32[1,2,128,4096]{3,2,1,0:T(8,128)} custom-call(f32[16,1,2,128,256]{4,3,2,1,0:T(8,128)} %all-to-all-done.x_ref, f32[16,2,8,256]{3,2,1,0:T(8,128)} %constant.51.clone.twist_ref, bf16[2,512,256]{2,1,0:T(8,128)(2,1)} %constant.53.clone.table_ref), custom_call_target="tpu_custom_call" | custom-call | tf_op jit(solution)/shard_map/column_forward/pallas_call | solution.py:393
  294.6 32.0 %column_forward.4.w1_ref.w2_ref.w3_ref = f32[3,2,64,4096]{3,2,1,0:T(8,128)} custom-call(f32[16,3,2,64,256]{4,3,2,1,0:T(8,128)} %all_to_all.30.x_ref, f32[16,2,8,256]{3,2,1,0:T(8,128)} %constant.51.clone.twist_ref, bf16[2,512,256]{2,1,0:T(8,128)(2,1)} %constant.53.clone.table_ref), custom_call_target="tpu_custom_call" | custom-call | tf_op jit(solution)/shard_map/column_forward/pallas_call | solution.py:393
  326.6 79.9 %column_inverse.2 = (f32[16,3,256,128]{3,2,1,0:T(8,128)}, f32[16,1,256,128]{3,2,1,0:T(8,128)}) custom-call(f32[1,2,128,4096]{3,2,1,0:T(8,128)} %column_forward.3.w0_ref, f32[3,2,64,4096]{3,2,1,0:T(8,128)} %column_forward.4.w1_ref.w2_ref.w3_ref, f32[3,2,64,4096]{3,2,1,0:T(8,128)} %column_forward.4.w1_ref.w2_ref.w3_ref, ...), custom_call_target="tpu_custom_call" | custom-call | tf_op jit(solution)/shard_map/column_inverse/pallas_call | solution.py:428
  406.5 2.9 all-to-all-done.2.x_ref
  409.4 5.2 all-to-all-start.3
  414.6 32.0 %column_forward.5.w1_ref.w2_ref.w3_ref = f32[3,2,64,4096]{3,2,1,0:T(8,128)} custom-call(f32[16,3,2,64,256]{4,3,2,1,0:T(8,128)} %all-to-all-done.2.x_ref, f32[16,2,8,256]{3,2,1,0:T(8,128)} %constant.51.clone.twist_ref, bf16[2,512,256]{2,1,0:T(8,128)(2,1)} %constant.53.clone.table_ref), custom_call_target="tpu_custom_call" | custom-call | tf_op jit(solution)/shard_map/column_forward/pallas_call | solution.py:393
  446.6 79.8 %column_inverse.3 = (f32[16,3,256,128]{3,2,1,0:T(8,128)}, f32[16,1,256,128]{3,2,1,0:T(8,128)}) custom-call(f32[1,2,128,4096]{3,2,1,0:T(8,128)} %column_forward.3.w0_ref, f32[3,2,64,4096]{3,2,1,0:T(8,128)} %column_forward.5.w1_ref.w2_ref.w3_ref, f32[3,2,64,4096]{3,2,1,0:T(8,128)} %column_forward.5.w1_ref.w2_ref.w3_ref, ...), custom_call_target="tpu_custom_call" | custom-call | tf_op jit(solution)/shard_map/column_inverse/pallas_call | solution.py:428
  526.4 25.3 %all-to-all-done.3.low_ref = f32[16,3,256,128]{3,2,1,0:T(8,128)} async-done(((f32[16,3,256,128]{3,2,1,0:T(8,128)}), f32[16,3,256,128]{3,2,1,0:T(8,128)}, u32[]{:S(2)}, u32[]{:S(2)}) %all-to-all-start.3) | async-done | bytes 6291488 | tf_op jit(solution)/shard_map/all_to_all | solution.py:632
  551.7 5.3 all-to-all-start.4
  557.0 3.9 pad_maximum_fusion
  561.0 133.2 %all-to-all-done.4.high_ref = f32[16,3,256,128]{3,2,1,0:T(8,128)} async-done(((f32[16,3,256,128]{3,2,1,0:T(8,128)}), f32[16,3,256,128]{3,2,1,0:T(8,128)}, u32[]{:S(2)}, u32[]{:S(2)}) %all-to-all-start.4) | async-done | bytes 6291488 | tf_op jit(solution)/shard_map/all_to_all | solution.py:632
  694.2 5.2 all-to-all-start.5
  699.4 77.8 %row_inverse.2 = (f32[4,512,2048]{2,1,0:T(8,128)}, f32[3,256,2048]{2,1,0:T(8,128)}) custom-call(s32[1]{0:T(128)} %bitcast.core_ref, f32[16,3,256,128]{3,2,1,0:T(8,128)} %all-to-all-done.3.low_ref, f32[16,3,256,128]{3,2,1,0:T(8,128)} %all-to-all-done.4.high_ref, f32[32,2,8,128]{3,2,1,0:T(8,128)} %constant.56.clone.twist_ref, ...), custom_call_target="tpu_custom_call" | custom-call | tf_op jit(solution)/shard_map/row_inverse/pallas_call | solution.py:464
  777.5 10.0 %collective-permute-done.2 = f32[3,256,2048]{2,1,0:T(8,128)S(1)} collective-permute-done((f32[3,256,2048]{2,1,0:T(8,128)}, f32[3,256,2048]{2,1,0:T(8,128)S(1)}, u32[]{:S(2)}, u32[]{:S(2)}) %collective-permute-start.2) | collective-permute-done | bytes 6291488 | tf_op jit(solution)/shard_map/ppermute | solution.py:623
  787.6 3.1 constant_dynamic-update-slice_fusion.1.refs_0_
  791.5 27.8 %row_inverse.3 = (f32[4,512,2048]{2,1,0:T(8,128)}, f32[1,256,2048]{2,1,0:T(8,128)}) custom-call(s32[1]{0:T(128)} %bitcast.core_ref, f32[16,2,256,128]{3,2,1,0:T(8,128)} %all-to-all-done.5.low_ref.high_ref, f32[16,2,256,128]{3,2,1,0:T(8,128)} %all-to-all-done.5.low_ref.high_ref, ...), custom_call_target="tpu_custom_call", output_to_operand_aliasing={{0}: (5, {})} | custom-call | tf_op jit(solution)/shard_map/row_inverse/pallas_call | solution.py:464
  819.4 0.9 collective-permute-start.3
  820.3 4.0 collective-permute-done.3
  824.3 1.5 constant_dynamic-update-slice_fusion
  (9 shorter events, 2.3 us)
Async XLA Ops:
  3.1 4.7 collective-permute-start
  7.8 1.3 copy-start.1
  25.9 98.4 %all-to-all-start = ((f32[16,1,2,128,256]{4,3,2,1,0:T(8,128)}), f32[16,1,2,128,256]{4,3,2,1,0:T(8,128)}, u32[]{:S(2)}, u32[]{:S(2)}) async-start(f32[16,1,2,128,256]{4,3,2,1,0:T(8,128)} %row_forward.2), calls=%async_computation | async-start | bytes 8388608 | tf_op jit(solution)/shard_map/all_to_all | solution.py:632
  35.3 10.2 %collective-permute-start.1 = (f32[3,256,2048]{2,1,0:T(8,128)S(1)}, f32[3,256,2048]{2,1,0:T(8,128)S(1)}, u32[]{:S(2)}, u32[]{:S(2)}) collective-permute-start(f32[3,256,2048]{2,1,0:T(8,128)S(1)} %constant_dynamic-slice_fusion), channel_id=1, source_target_pairs={{0,1},{1,0},{2,3},{3,2},{4,5},{5,4},{6,7},{7,6},{8,9},{9,8},{10,11... | collective-permute-start | bytes 18874376 | tf_op jit(solution)/shard_map/ppermute | solution.py:623
  45.5 2.7 copy-start
  266.5 142.9 %all-to-all-start.2 = ((f32[16,3,2,64,256]{4,3,2,1,0:T(8,128)}), f32[16,3,2,64,256]{4,3,2,1,0:T(8,128)}, u32[]{:S(2)}, u32[]{:S(2)}) async-start(f32[16,3,2,64,256]{4,3,2,1,0:T(8,128)} %get-tuple-element.34), calls=%async_computation.2 | async-start | bytes 12582912 | tf_op jit(solution)/shard_map/all_to_all | solution.py:632
  409.4 142.3 %all-to-all-start.3 = ((f32[16,3,256,128]{3,2,1,0:T(8,128)}), f32[16,3,256,128]{3,2,1,0:T(8,128)}, u32[]{:S(2)}, u32[]{:S(2)}) async-start(f32[16,3,256,128]{3,2,1,0:T(8,128)} %get-tuple-element.38), calls=%async_computation.3 | async-start | bytes 12582912 | tf_op jit(solution)/shard_map/all_to_all | solution.py:632
  551.7 5.3 copy-start.2
  551.7 142.4 %all-to-all-start.4 = ((f32[16,3,256,128]{3,2,1,0:T(8,128)}), f32[16,3,256,128]{3,2,1,0:T(8,128)}, u32[]{:S(2)}, u32[]{:S(2)}) async-start(f32[16,3,256,128]{3,2,1,0:T(8,128)} %get-tuple-element.39), calls=%async_computation.4 | async-start | bytes 12582912 | tf_op jit(solution)/shard_map/all_to_all | solution.py:632
  694.2 97.4 %all-to-all-start.5 = ((f32[16,2,256,128]{3,2,1,0:T(8,128)}), f32[16,2,256,128]{3,2,1,0:T(8,128)}, u32[]{:S(2)}, u32[]{:S(2)}) async-start(f32[16,2,256,128]{3,2,1,0:T(8,128)} %pad_maximum_fusion), calls=%async_computation.5 | async-start | bytes 8388608 | tf_op jit(solution)/shard_map/all_to_all | solution.py:632
  777.2 10.4 %collective-permute-start.2 = (f32[3,256,2048]{2,1,0:T(8,128)}, f32[3,256,2048]{2,1,0:T(8,128)S(1)}, u32[]{:S(2)}, u32[]{:S(2)}) collective-permute-start(f32[3,256,2048]{2,1,0:T(8,128)} %get-tuple-element.44), channel_id=1, source_target_pairs={{0,1},{1,0},{2,3},{3,2},{4,5},{5,4},{6,7},{7,6},{8,9},{9,8},{10,11... | collective-permute-start | bytes 18874376 | tf_op jit(solution)/shard_map/ppermute | solution.py:623
  819.4 4.9 collective-permute-start.3

commit v3 on v2

--- a/solution.py
+++ b/solution.py
@@ -181,7 +181,7 @@
                     ]
         return 0
 
-    lax.fori_loop(0, RADIX, line, 0)
+    lax.fori_loop(0, RADIX, line, 0, unroll=2)
 
 
 def complex_lines(read, rows, width, sign, twist_ref, part_ref):
@@ -217,7 +217,7 @@
         )
         return 0
 
-    lax.fori_loop(0, RADIX, line, 0)
+    lax.fori_loop(0, RADIX, line, 0, unroll=2)
 
     def flip(index, _):
         start = pl.multiple_of(index * width, width)
@@ -273,7 +273,7 @@
                     ]
                 return 0
 
-            lax.fori_loop(0, RADIX, line, 0)
+            lax.fori_loop(0, RADIX, line, 0, unroll=2)
 
         first = 0
         for count, out_ref in zip(counts, out_refs):
@@ -320,7 +320,7 @@
         order_ref[pl.ds(index, out_len, stride=count), :] = matmul_split(table_ref, part_ref[index])
         return 0
 
-    lax.fori_loop(0, count, line, 0)
+    lax.fori_loop(0, count, line, 0, unroll=4)
     half_len = sent_ref.shape[2]
     chunk = 256
     own = core_ref[0] * half_len

time: 828 us -> 815 us (0.984)
  Pallas kernels: 414 us -> 329 us
  waiting for transfers between devices: 219 us -> 291 us
    all_to_all x5, waiting for transfers between devices: 193 us -> 265 us  [exchange_all(): lax.all_to_all(values, ('row', 'col'), split_axis=0, concat_axis=0, tiled...]
    pallas_call x2, Pallas kernels: 106 us -> 65.4 us  [row_inverse(): pl.pallas_call(row_inverse_kernel, grid_spec=pltpu.PrefetchScalarGridSpec...]
    pallas_call x3, Pallas kernels: 86.3 us -> 71.2 us  [column_forward(): pl.pallas_call(column_forward_kernel, grid=(count, rows // PACKED), in_sp...]
    pallas_call x2, Pallas kernels: 160 us -> 145 us  [column_inverse(): pl.pallas_call(functools.partial(column_inverse_kernel, counts), grid=(su...]
    pallas_call x2, Pallas kernels: 61.9 us -> 47.4 us  [row_forward(): pl.pallas_call(row_forward_kernel, grid_spec=pltpu.PrefetchScalarGridSpec...]
  transfers between devices with their start and end apart: 9 -> 9, of which waited for: 9 -> 9; matrix products, arithmetic and copies ran while one was open for 1% -> 1% of each run, Pallas kernels for 45% -> 37%
where the time goes in v3:
time: 815 us; the launch traced here: 812 us
  Pallas kernels  329 us (40%)
  waiting for transfers between devices  291 us (36%)
  blocking collectives  142 us (17%)
  starting transfers between devices  29.9 us (4%)
  local copies, waits for them, and re-layouts  15 us (2%)
    all_to_all x5, waiting for transfers between devices, exchange_all(): lax.all_to_all(values, ('row', 'col'), split_axis=0, concat_axis=0, tiled...  265 us
    pallas_call x2, Pallas kernels, column_inverse(): pl.pallas_call(functools.partial(column_inverse_kernel, counts), grid=(su...  145 us
    all_to_all x1, blocking collectives, exchange_all(): lax.all_to_all(values, ('row', 'col'), split_axis=0, concat_axis=0, tiled...  142 us
    pallas_call x3, Pallas kernels, column_forward(): pl.pallas_call(column_forward_kernel, grid=(count, rows // PACKED), in_sp...  71.2 us
    pallas_call x2, Pallas kernels, row_inverse(): pl.pallas_call(row_inverse_kernel, grid_spec=pltpu.PrefetchScalarGridSpec...  65.4 us
    pallas_call x2, Pallas kernels, row_forward(): pl.pallas_call(row_forward_kernel, grid_spec=pltpu.PrefetchScalarGridSpec...  47.4 us
    all_to_all x5, starting transfers between devices, exchange_all(): lax.all_to_all(values, ('row', 'col'), split_axis=0, concat_axis=0, tiled...  27.6 us
    ppermute x4, waiting for transfers between devices, swap_cores(): return lax.ppermute(values, 'col', [(0, 1), (1, 0)])  26 us
  transfers between devices with their start and end apart: 9, of which 9 were waited for; matrix products, arithmetic and copies ran while one was open for 1% of the time, Pallas kernels for 37%

profile of v3, /device:TPU:17, one launch (start us, length us, event | category | flops | bytes accessed | tf_op | source)
XLA Modules:
  0.0 812.1 jit_solution(13117321426143507905)
XLA Ops:
  0.0 3.1 constant_dynamic-slice_fusion.1
  3.8 1.7 broadcast_multiply_fusion.twist_ref
  5.6 2.3 collective-permute-done.other_ref
  7.8 1.3 copy-done.1
  9.1 13.3 %row_forward.2 = f32[16,1,2,128,256]{4,3,2,1,0:T(8,128)} custom-call(s32[1]{0:T(128)} %bitcast.core_ref, f32[4,512,2048]{2,1,0:T(8,128)} %own_ref.3, f32[1,256,2048]{2,1,0:T(8,128)} %copy-done.1, f32[16,2,8,256]{3,2,1,0:T(8,128)} %broadcast_multiply_fusion.twist_ref, bf16[2,256,256]{2,1,0:T(8,128)(2,1)} %constant.52.clone.table_ref), custom_call_target="tpu_custom_call" | custom-call | tf_op jit(solution)/shard_map/row_forward/pallas_call | solution.py:363
  22.4 6.2 all-to-all-start
  28.6 3.2 constant_dynamic-slice_fusion
  32.2 9.8 %collective-permute-done.1.other_ref = f32[3,256,2048]{2,1,0:T(8,128)S(1)} collective-permute-done((f32[3,256,2048]{2,1,0:T(8,128)S(1)}, f32[3,256,2048]{2,1,0:T(8,128)S(1)}, u32[]{:S(2)}, u32[]{:S(2)}) %collective-permute-start.1) | collective-permute-done | bytes 6291488 | tf_op jit(solution)/shard_map/ppermute | solution.py:623
  42.0 2.7 copy-done
  44.7 34.1 %row_forward.3 = (f32[16,3,2,64,256]{4,3,2,1,0:T(8,128)}, f32[16,3,2,64,256]{4,3,2,1,0:T(8,128)}) custom-call(s32[1]{0:T(128)} %bitcast.core_ref, f32[4,512,2048]{2,1,0:T(8,128)} %own_ref.3, f32[3,256,2048]{2,1,0:T(8,128)} %copy-done, f32[16,2,8,256]{3,2,1,0:T(8,128)} %broadcast_multiply_fusion.twist_ref, bf16[2,256,256]{2,1,0:T(8,128)(2,1)} %constant.52.clone.table_ref), custom_call_target="tpu_custom_call" | custom-call | tf_op jit(solution)/shard_map/row_forward/pallas_call | solution.py:363
  78.8 41.9 %all-to-all-done.x_ref = f32[16,1,2,128,256]{4,3,2,1,0:T(8,128)} async-done(((f32[16,1,2,128,256]{4,3,2,1,0:T(8,128)}), f32[16,1,2,128,256]{4,3,2,1,0:T(8,128)}, u32[]{:S(2)}, u32[]{:S(2)}) %all-to-all-start) | async-done | bytes 4194336 | tf_op jit(solution)/shard_map/all_to_all | solution.py:632
  120.7 142.2 %all_to_all.30.x_ref = f32[16,3,2,64,256]{4,3,2,1,0:T(8,128)} all-to-all(f32[16,3,2,64,256]{4,3,2,1,0:T(8,128)} %get-tuple-element.31), channel_id=1, replica_groups=mesh['tiles'=2,'row'=8,'col'=2] {'row','col'}, dimensions={0} | all-to-all | bytes 12582912 | tf_op jit(solution)/shard_map/all_to_all | solution.py:632
  263.0 5.7 all-to-all-start.2
  268.7 18.6 %column_forward.3.w0_ref = f32[1,2,128,4096]{3,2,1,0:T(8,128)} custom-call(f32[16,1,2,128,256]{4,3,2,1,0:T(8,128)} %all-to-all-done.x_ref, f32[16,2,8,256]{3,2,1,0:T(8,128)} %constant.51.clone.twist_ref, bf16[2,512,256]{2,1,0:T(8,128)(2,1)} %constant.53.clone.table_ref), custom_call_target="tpu_custom_call" | custom-call | tf_op jit(solution)/shard_map/column_forward/pallas_call | solution.py:393
  287.3 26.3 %column_forward.4.w1_ref.w2_ref.w3_ref = f32[3,2,64,4096]{3,2,1,0:T(8,128)} custom-call(f32[16,3,2,64,256]{4,3,2,1,0:T(8,128)} %all_to_all.30.x_ref, f32[16,2,8,256]{3,2,1,0:T(8,128)} %constant.51.clone.twist_ref, bf16[2,512,256]{2,1,0:T(8,128)(2,1)} %constant.53.clone.table_ref), custom_call_target="tpu_custom_call" | custom-call | tf_op jit(solution)/shard_map/column_forward/pallas_call | solution.py:393
  313.6 72.4 %column_inverse.2 = (f32[16,3,256,128]{3,2,1,0:T(8,128)}, f32[16,1,256,128]{3,2,1,0:T(8,128)}) custom-call(f32[1,2,128,4096]{3,2,1,0:T(8,128)} %column_forward.3.w0_ref, f32[3,2,64,4096]{3,2,1,0:T(8,128)} %column_forward.4.w1_ref.w2_ref.w3_ref, f32[3,2,64,4096]{3,2,1,0:T(8,128)} %column_forward.4.w1_ref.w2_ref.w3_ref, ...), custom_call_target="tpu_custom_call" | custom-call | tf_op jit(solution)/shard_map/column_inverse/pallas_call | solution.py:428
  386.0 19.9 %all-to-all-done.2.x_ref = f32[16,3,2,64,256]{4,3,2,1,0:T(8,128)} async-done(((f32[16,3,2,64,256]{4,3,2,1,0:T(8,128)}), f32[16,3,2,64,256]{4,3,2,1,0:T(8,128)}, u32[]{:S(2)}, u32[]{:S(2)}) %all-to-all-start.2) | async-done | bytes 6291488 | tf_op jit(solution)/shard_map/all_to_all | solution.py:632
  405.9 5.2 all-to-all-start.3
  411.0 26.3 %column_forward.5.w1_ref.w2_ref.w3_ref = f32[3,2,64,4096]{3,2,1,0:T(8,128)} custom-call(f32[16,3,2,64,256]{4,3,2,1,0:T(8,128)} %all-to-all-done.2.x_ref, f32[16,2,8,256]{3,2,1,0:T(8,128)} %constant.51.clone.twist_ref, bf16[2,512,256]{2,1,0:T(8,128)(2,1)} %constant.53.clone.table_ref), custom_call_target="tpu_custom_call" | custom-call | tf_op jit(solution)/shard_map/column_forward/pallas_call | solution.py:393
  437.4 72.3 %column_inverse.3 = (f32[16,3,256,128]{3,2,1,0:T(8,128)}, f32[16,1,256,128]{3,2,1,0:T(8,128)}) custom-call(f32[1,2,128,4096]{3,2,1,0:T(8,128)} %column_forward.3.w0_ref, f32[3,2,64,4096]{3,2,1,0:T(8,128)} %column_forward.5.w1_ref.w2_ref.w3_ref, f32[3,2,64,4096]{3,2,1,0:T(8,128)} %column_forward.5.w1_ref.w2_ref.w3_ref, ...), custom_call_target="tpu_custom_call" | custom-call | tf_op jit(solution)/shard_map/column_inverse/pallas_call | solution.py:428
  509.7 38.5 %all-to-all-done.3.low_ref = f32[16,3,256,128]{3,2,1,0:T(8,128)} async-done(((f32[16,3,256,128]{3,2,1,0:T(8,128)}), f32[16,3,256,128]{3,2,1,0:T(8,128)}, u32[]{:S(2)}, u32[]{:S(2)}) %all-to-all-start.3) | async-done | bytes 6291488 | tf_op jit(solution)/shard_map/all_to_all | solution.py:632
  548.2 5.3 all-to-all-start.4
  553.5 3.9 pad_maximum_fusion
  557.4 133.2 %all-to-all-done.4.high_ref = f32[16,3,256,128]{3,2,1,0:T(8,128)} async-done(((f32[16,3,256,128]{3,2,1,0:T(8,128)}), f32[16,3,256,128]{3,2,1,0:T(8,128)}, u32[]{:S(2)}, u32[]{:S(2)}) %all-to-all-start.4) | async-done | bytes 6291488 | tf_op jit(solution)/shard_map/all_to_all | solution.py:632
  690.6 5.2 all-to-all-start.5
  695.8 47.6 %row_inverse.2 = (f32[4,512,2048]{2,1,0:T(8,128)}, f32[3,256,2048]{2,1,0:T(8,128)}) custom-call(s32[1]{0:T(128)} %bitcast.core_ref, f32[16,3,256,128]{3,2,1,0:T(8,128)} %all-to-all-done.3.low_ref, f32[16,3,256,128]{3,2,1,0:T(8,128)} %all-to-all-done.4.high_ref, f32[32,2,8,128]{3,2,1,0:T(8,128)} %constant.56.clone.twist_ref, ...), custom_call_target="tpu_custom_call" | custom-call | tf_op jit(solution)/shard_map/row_inverse/pallas_call | solution.py:464
  743.8 10.0 %collective-permute-done.2 = f32[3,256,2048]{2,1,0:T(8,128)S(1)} collective-permute-done((f32[3,256,2048]{2,1,0:T(8,128)}, f32[3,256,2048]{2,1,0:T(8,128)S(1)}, u32[]{:S(2)}, u32[]{:S(2)}) %collective-permute-start.2) | collective-permute-done | bytes 6291488 | tf_op jit(solution)/shard_map/ppermute | solution.py:623
  753.8 3.1 constant_dynamic-update-slice_fusion.1.refs_0_
  756.9 31.1 %all-to-all-done.5.low_ref.high_ref = f32[16,2,256,128]{3,2,1,0:T(8,128)} async-done(((f32[16,2,256,128]{3,2,1,0:T(8,128)}), f32[16,2,256,128]{3,2,1,0:T(8,128)}, u32[]{:S(2)}, u32[]{:S(2)}) %all-to-all-start.5) | async-done | bytes 4194336 | tf_op jit(solution)/shard_map/all_to_all | solution.py:632
  788.0 17.8 %row_inverse.3 = (f32[4,512,2048]{2,1,0:T(8,128)}, f32[1,256,2048]{2,1,0:T(8,128)}) custom-call(s32[1]{0:T(128)} %bitcast.core_ref, f32[16,2,256,128]{3,2,1,0:T(8,128)} %all-to-all-done.5.low_ref.high_ref, f32[16,2,256,128]{3,2,1,0:T(8,128)} %all-to-all-done.5.low_ref.high_ref, ...), custom_call_target="tpu_custom_call", output_to_operand_aliasing={{0}: (5, {})} | custom-call | tf_op jit(solution)/shard_map/row_inverse/pallas_call | solution.py:464
  806.6 4.0 collective-permute-done.3
  810.6 1.5 constant_dynamic-update-slice_fusion
  (9 shorter events, 2.4 us)
Async XLA Ops:
  3.1 4.7 collective-permute-start
  7.8 1.3 copy-start.1
  22.4 98.3 %all-to-all-start = ((f32[16,1,2,128,256]{4,3,2,1,0:T(8,128)}), f32[16,1,2,128,256]{4,3,2,1,0:T(8,128)}, u32[]{:S(2)}, u32[]{:S(2)}) async-start(f32[16,1,2,128,256]{4,3,2,1,0:T(8,128)} %row_forward.2), calls=%async_computation | async-start | bytes 8388608 | tf_op jit(solution)/shard_map/all_to_all | solution.py:632
  31.8 10.2 %collective-permute-start.1 = (f32[3,256,2048]{2,1,0:T(8,128)S(1)}, f32[3,256,2048]{2,1,0:T(8,128)S(1)}, u32[]{:S(2)}, u32[]{:S(2)}) collective-permute-start(f32[3,256,2048]{2,1,0:T(8,128)S(1)} %constant_dynamic-slice_fusion), channel_id=1, source_target_pairs={{0,1},{1,0},{2,3},{3,2},{4,5},{5,4},{6,7},{7,6},{8,9},{9,8},{10,11... | collective-permute-start | bytes 18874376 | tf_op jit(solution)/shard_map/ppermute | solution.py:623
  42.0 2.7 copy-start
  263.0 142.9 %all-to-all-start.2 = ((f32[16,3,2,64,256]{4,3,2,1,0:T(8,128)}), f32[16,3,2,64,256]{4,3,2,1,0:T(8,128)}, u32[]{:S(2)}, u32[]{:S(2)}) async-start(f32[16,3,2,64,256]{4,3,2,1,0:T(8,128)} %get-tuple-element.34), calls=%async_computation.2 | async-start | bytes 12582912 | tf_op jit(solution)/shard_map/all_to_all | solution.py:632
  405.9 142.3 %all-to-all-start.3 = ((f32[16,3,256,128]{3,2,1,0:T(8,128)}), f32[16,3,256,128]{3,2,1,0:T(8,128)}, u32[]{:S(2)}, u32[]{:S(2)}) async-start(f32[16,3,256,128]{3,2,1,0:T(8,128)} %get-tuple-element.38), calls=%async_computation.3 | async-start | bytes 12582912 | tf_op jit(solution)/shard_map/all_to_all | solution.py:632
  548.2 5.3 copy-start.2
  548.2 142.4 %all-to-all-start.4 = ((f32[16,3,256,128]{3,2,1,0:T(8,128)}), f32[16,3,256,128]{3,2,1,0:T(8,128)}, u32[]{:S(2)}, u32[]{:S(2)}) async-start(f32[16,3,256,128]{3,2,1,0:T(8,128)} %get-tuple-element.39), calls=%async_computation.4 | async-start | bytes 12582912 | tf_op jit(solution)/shard_map/all_to_all | solution.py:632
  690.6 97.4 %all-to-all-start.5 = ((f32[16,2,256,128]{3,2,1,0:T(8,128)}), f32[16,2,256,128]{3,2,1,0:T(8,128)}, u32[]{:S(2)}, u32[]{:S(2)}) async-start(f32[16,2,256,128]{3,2,1,0:T(8,128)} %pad_maximum_fusion), calls=%async_computation.5 | async-start | bytes 8388608 | tf_op jit(solution)/shard_map/all_to_all | solution.py:632
  743.4 10.4 %collective-permute-start.2 = (f32[3,256,2048]{2,1,0:T(8,128)}, f32[3,256,2048]{2,1,0:T(8,128)S(1)}, u32[]{:S(2)}, u32[]{:S(2)}) collective-permute-start(f32[3,256,2048]{2,1,0:T(8,128)} %get-tuple-element.44), channel_id=1, source_target_pairs={{0,1},{1,0},{2,3},{3,2},{4,5},{5,4},{6,7},{7,6},{8,9},{9,8},{10,11... | collective-permute-start | bytes 18874376 | tf_op jit(solution)/shard_map/ppermute | solution.py:623
  805.8 4.9 collective-permute-start.3

commit v4 on v3

--- a/solution.py
+++ b/solution.py
@@ -181,7 +181,7 @@
                     ]
         return 0
 
-    lax.fori_loop(0, RADIX, line, 0, unroll=2)
+    lax.fori_loop(0, RADIX, line, 0, unroll=4)
 
 
 def complex_lines(read, rows, width, sign, twist_ref, part_ref):

time: 815 us -> 813 us (level)
  transfers between devices with their start and end apart: 9 -> 9, of which waited for: 9 -> 9; matrix products, arithmetic and copies ran while one was open for 1% -> 1% of each run, Pallas kernels for 37% -> 36%
where the time goes in v4:
time: 813 us; the launch traced here: 811 us
  Pallas kernels  322 us (40%)
  waiting for transfers between devices  295 us (36%)
  blocking collectives  142 us (17%)
  starting transfers between devices  29.9 us (4%)
  local copies, waits for them, and re-layouts  15 us (2%)
    all_to_all x5, waiting for transfers between devices, exchange_all(): lax.all_to_all(values, ('row', 'col'), split_axis=0, concat_axis=0, tiled...  269 us
    pallas_call x2, Pallas kernels, column_inverse(): pl.pallas_call(functools.partial(column_inverse_kernel, counts), grid=(su...  145 us
    all_to_all x1, blocking collectives, exchange_all(): lax.all_to_all(values, ('row', 'col'), split_axis=0, concat_axis=0, tiled...  142 us
    pallas_call x3, Pallas kernels, column_forward(): pl.pallas_call(column_forward_kernel, grid=(count, rows // PACKED), in_sp...  71.2 us
    pallas_call x2, Pallas kernels, row_inverse(): pl.pallas_call(row_inverse_kernel, grid_spec=pltpu.PrefetchScalarGridSpec...  65.4 us
    pallas_call x2, Pallas kernels, row_forward(): pl.pallas_call(row_forward_kernel, grid_spec=pltpu.PrefetchScalarGridSpec...  41.1 us
    all_to_all x5, starting transfers between devices, exchange_all(): lax.all_to_all(values, ('row', 'col'), split_axis=0, concat_axis=0, tiled...  27.6 us
    ppermute x4, waiting for transfers between devices, swap_cores(): return lax.ppermute(values, 'col', [(0, 1), (1, 0)])  26.1 us
  transfers between devices with their start and end apart: 9, of which 9 were waited for; matrix products, arithmetic and copies ran while one was open for 1% of the time, Pallas kernels for 36%

profile of v4, /device:TPU:17, one launch (start us, length us, event | category | flops | bytes accessed | tf_op | source)
XLA Modules:
  0.0 810.6 jit_solution(4357775987799937823)
XLA Ops:
  0.0 3.1 constant_dynamic-slice_fusion.1
  3.8 1.7 broadcast_multiply_fusion.twist_ref
  5.6 2.3 collective-permute-done.other_ref
  7.8 1.3 copy-done.1
  9.1 11.8 %row_forward.2 = f32[16,1,2,128,256]{4,3,2,1,0:T(8,128)} custom-call(s32[1]{0:T(128)} %bitcast.core_ref, f32[4,512,2048]{2,1,0:T(8,128)} %own_ref.3, f32[1,256,2048]{2,1,0:T(8,128)} %copy-done.1, f32[16,2,8,256]{3,2,1,0:T(8,128)} %broadcast_multiply_fusion.twist_ref, bf16[2,256,256]{2,1,0:T(8,128)(2,1)} %constant.52.clone.table_ref), custom_call_target="tpu_custom_call" | custom-call | tf_op jit(solution)/shard_map/row_forward/pallas_call | solution.py:363
  20.9 6.2 all-to-all-start
  27.1 3.2 constant_dynamic-slice_fusion
  30.7 9.8 %collective-permute-done.1.other_ref = f32[3,256,2048]{2,1,0:T(8,128)S(1)} collective-permute-done((f32[3,256,2048]{2,1,0:T(8,128)S(1)}, f32[3,256,2048]{2,1,0:T(8,128)S(1)}, u32[]{:S(2)}, u32[]{:S(2)}) %collective-permute-start.1) | collective-permute-done | bytes 6291488 | tf_op jit(solution)/shard_map/ppermute | solution.py:623
  40.5 2.7 copy-done
  43.2 29.3 %row_forward.3 = (f32[16,3,2,64,256]{4,3,2,1,0:T(8,128)}, f32[16,3,2,64,256]{4,3,2,1,0:T(8,128)}) custom-call(s32[1]{0:T(128)} %bitcast.core_ref, f32[4,512,2048]{2,1,0:T(8,128)} %own_ref.3, f32[3,256,2048]{2,1,0:T(8,128)} %copy-done, f32[16,2,8,256]{3,2,1,0:T(8,128)} %broadcast_multiply_fusion.twist_ref, bf16[2,256,256]{2,1,0:T(8,128)(2,1)} %constant.52.clone.table_ref), custom_call_target="tpu_custom_call" | custom-call | tf_op jit(solution)/shard_map/row_forward/pallas_call | solution.py:363
  72.5 46.7 %all-to-all-done.x_ref = f32[16,1,2,128,256]{4,3,2,1,0:T(8,128)} async-done(((f32[16,1,2,128,256]{4,3,2,1,0:T(8,128)}), f32[16,1,2,128,256]{4,3,2,1,0:T(8,128)}, u32[]{:S(2)}, u32[]{:S(2)}) %all-to-all-start) | async-done | bytes 4194336 | tf_op jit(solution)/shard_map/all_to_all | solution.py:632
  119.3 142.2 %all_to_all.30.x_ref = f32[16,3,2,64,256]{4,3,2,1,0:T(8,128)} all-to-all(f32[16,3,2,64,256]{4,3,2,1,0:T(8,128)} %get-tuple-element.31), channel_id=1, replica_groups=mesh['tiles'=2,'row'=8,'col'=2] {'row','col'}, dimensions={0} | all-to-all | bytes 12582912 | tf_op jit(solution)/shard_map/all_to_all | solution.py:632
  261.5 5.7 all-to-all-start.2
  267.2 18.6 %column_forward.3.w0_ref = f32[1,2,128,4096]{3,2,1,0:T(8,128)} custom-call(f32[16,1,2,128,256]{4,3,2,1,0:T(8,128)} %all-to-all-done.x_ref, f32[16,2,8,256]{3,2,1,0:T(8,128)} %constant.51.clone.twist_ref, bf16[2,512,256]{2,1,0:T(8,128)(2,1)} %constant.53.clone.table_ref), custom_call_target="tpu_custom_call" | custom-call | tf_op jit(solution)/shard_map/column_forward/pallas_call | solution.py:393
  285.8 26.3 %column_forward.4.w1_ref.w2_ref.w3_ref = f32[3,2,64,4096]{3,2,1,0:T(8,128)} custom-call(f32[16,3,2,64,256]{4,3,2,1,0:T(8,128)} %all_to_all.30.x_ref, f32[16,2,8,256]{3,2,1,0:T(8,128)} %constant.51.clone.twist_ref, bf16[2,512,256]{2,1,0:T(8,128)(2,1)} %constant.53.clone.table_ref), custom_call_target="tpu_custom_call" | custom-call | tf_op jit(solution)/shard_map/column_forward/pallas_call | solution.py:393
  312.1 72.4 %column_inverse.2 = (f32[16,3,256,128]{3,2,1,0:T(8,128)}, f32[16,1,256,128]{3,2,1,0:T(8,128)}) custom-call(f32[1,2,128,4096]{3,2,1,0:T(8,128)} %column_forward.3.w0_ref, f32[3,2,64,4096]{3,2,1,0:T(8,128)} %column_forward.4.w1_ref.w2_ref.w3_ref, f32[3,2,64,4096]{3,2,1,0:T(8,128)} %column_forward.4.w1_ref.w2_ref.w3_ref, ...), custom_call_target="tpu_custom_call" | custom-call | tf_op jit(solution)/shard_map/column_inverse/pallas_call | solution.py:428
  384.5 19.9 %all-to-all-done.2.x_ref = f32[16,3,2,64,256]{4,3,2,1,0:T(8,128)} async-done(((f32[16,3,2,64,256]{4,3,2,1,0:T(8,128)}), f32[16,3,2,64,256]{4,3,2,1,0:T(8,128)}, u32[]{:S(2)}, u32[]{:S(2)}) %all-to-all-start.2) | async-done | bytes 6291488 | tf_op jit(solution)/shard_map/all_to_all | solution.py:632
  404.4 5.2 all-to-all-start.3
  409.6 26.3 %column_forward.5.w1_ref.w2_ref.w3_ref = f32[3,2,64,4096]{3,2,1,0:T(8,128)} custom-call(f32[16,3,2,64,256]{4,3,2,1,0:T(8,128)} %all-to-all-done.2.x_ref, f32[16,2,8,256]{3,2,1,0:T(8,128)} %constant.51.clone.twist_ref, bf16[2,512,256]{2,1,0:T(8,128)(2,1)} %constant.53.clone.table_ref), custom_call_target="tpu_custom_call" | custom-call | tf_op jit(solution)/shard_map/column_forward/pallas_call | solution.py:393
  435.9 72.3 %column_inverse.3 = (f32[16,3,256,128]{3,2,1,0:T(8,128)}, f32[16,1,256,128]{3,2,1,0:T(8,128)}) custom-call(f32[1,2,128,4096]{3,2,1,0:T(8,128)} %column_forward.3.w0_ref, f32[3,2,64,4096]{3,2,1,0:T(8,128)} %column_forward.5.w1_ref.w2_ref.w3_ref, f32[3,2,64,4096]{3,2,1,0:T(8,128)} %column_forward.5.w1_ref.w2_ref.w3_ref, ...), custom_call_target="tpu_custom_call" | custom-call | tf_op jit(solution)/shard_map/column_inverse/pallas_call | solution.py:428
  508.2 38.5 %all-to-all-done.3.low_ref = f32[16,3,256,128]{3,2,1,0:T(8,128)} async-done(((f32[16,3,256,128]{3,2,1,0:T(8,128)}), f32[16,3,256,128]{3,2,1,0:T(8,128)}, u32[]{:S(2)}, u32[]{:S(2)}) %all-to-all-start.3) | async-done | bytes 6291488 | tf_op jit(solution)/shard_map/all_to_all | solution.py:632
  546.7 5.3 all-to-all-start.4
  552.0 3.9 pad_maximum_fusion
  556.0 133.2 %all-to-all-done.4.high_ref = f32[16,3,256,128]{3,2,1,0:T(8,128)} async-done(((f32[16,3,256,128]{3,2,1,0:T(8,128)}), f32[16,3,256,128]{3,2,1,0:T(8,128)}, u32[]{:S(2)}, u32[]{:S(2)}) %all-to-all-start.4) | async-done | bytes 6291488 | tf_op jit(solution)/shard_map/all_to_all | solution.py:632
  689.1 5.2 all-to-all-start.5
  694.3 47.6 %row_inverse.2 = (f32[4,512,2048]{2,1,0:T(8,128)}, f32[3,256,2048]{2,1,0:T(8,128)}) custom-call(s32[1]{0:T(128)} %bitcast.core_ref, f32[16,3,256,128]{3,2,1,0:T(8,128)} %all-to-all-done.3.low_ref, f32[16,3,256,128]{3,2,1,0:T(8,128)} %all-to-all-done.4.high_ref, f32[32,2,8,128]{3,2,1,0:T(8,128)} %constant.56.clone.twist_ref, ...), custom_call_target="tpu_custom_call" | custom-call | tf_op jit(solution)/shard_map/row_inverse/pallas_call | solution.py:464
  742.3 10.0 %collective-permute-done.2 = f32[3,256,2048]{2,1,0:T(8,128)S(1)} collective-permute-done((f32[3,256,2048]{2,1,0:T(8,128)}, f32[3,256,2048]{2,1,0:T(8,128)S(1)}, u32[]{:S(2)}, u32[]{:S(2)}) %collective-permute-start.2) | collective-permute-done | bytes 6291488 | tf_op jit(solution)/shard_map/ppermute | solution.py:623
  752.3 3.1 constant_dynamic-update-slice_fusion.1.refs_0_
  755.4 31.1 %all-to-all-done.5.low_ref.high_ref = f32[16,2,256,128]{3,2,1,0:T(8,128)} async-done(((f32[16,2,256,128]{3,2,1,0:T(8,128)}), f32[16,2,256,128]{3,2,1,0:T(8,128)}, u32[]{:S(2)}, u32[]{:S(2)}) %all-to-all-start.5) | async-done | bytes 4194336 | tf_op jit(solution)/shard_map/all_to_all | solution.py:632
  786.5 17.8 %row_inverse.3 = (f32[4,512,2048]{2,1,0:T(8,128)}, f32[1,256,2048]{2,1,0:T(8,128)}) custom-call(s32[1]{0:T(128)} %bitcast.core_ref, f32[16,2,256,128]{3,2,1,0:T(8,128)} %all-to-all-done.5.low_ref.high_ref, f32[16,2,256,128]{3,2,1,0:T(8,128)} %all-to-all-done.5.low_ref.high_ref, ...), custom_call_target="tpu_custom_call", output_to_operand_aliasing={{0}: (5, {})} | custom-call | tf_op jit(solution)/shard_map/row_inverse/pallas_call | solution.py:464
  805.2 4.0 collective-permute-done.3
  809.2 1.5 constant_dynamic-update-slice_fusion
  (9 shorter events, 2.3 us)
Async XLA Ops:
  3.1 4.7 collective-permute-start
  7.8 1.3 copy-start.1
  20.9 98.3 %all-to-all-start = ((f32[16,1,2,128,256]{4,3,2,1,0:T(8,128)}), f32[16,1,2,128,256]{4,3,2,1,0:T(8,128)}, u32[]{:S(2)}, u32[]{:S(2)}) async-start(f32[16,1,2,128,256]{4,3,2,1,0:T(8,128)} %row_forward.2), calls=%async_computation | async-start | bytes 8388608 | tf_op jit(solution)/shard_map/all_to_all | solution.py:632
  30.3 10.2 %collective-permute-start.1 = (f32[3,256,2048]{2,1,0:T(8,128)S(1)}, f32[3,256,2048]{2,1,0:T(8,128)S(1)}, u32[]{:S(2)}, u32[]{:S(2)}) collective-permute-start(f32[3,256,2048]{2,1,0:T(8,128)S(1)} %constant_dynamic-slice_fusion), channel_id=1, source_target_pairs={{0,1},{1,0},{2,3},{3,2},{4,5},{5,4},{6,7},{7,6},{8,9},{9,8},{10,11... | collective-permute-start | bytes 18874376 | tf_op jit(solution)/shard_map/ppermute | solution.py:623
  40.5 2.7 copy-start
  261.5 142.9 %all-to-all-start.2 = ((f32[16,3,2,64,256]{4,3,2,1,0:T(8,128)}), f32[16,3,2,64,256]{4,3,2,1,0:T(8,128)}, u32[]{:S(2)}, u32[]{:S(2)}) async-start(f32[16,3,2,64,256]{4,3,2,1,0:T(8,128)} %get-tuple-element.34), calls=%async_computation.2 | async-start | bytes 12582912 | tf_op jit(solution)/shard_map/all_to_all | solution.py:632
  404.4 142.3 %all-to-all-start.3 = ((f32[16,3,256,128]{3,2,1,0:T(8,128)}), f32[16,3,256,128]{3,2,1,0:T(8,128)}, u32[]{:S(2)}, u32[]{:S(2)}) async-start(f32[16,3,256,128]{3,2,1,0:T(8,128)} %get-tuple-element.38), calls=%async_computation.3 | async-start | bytes 12582912 | tf_op jit(solution)/shard_map/all_to_all | solution.py:632
  546.7 5.3 copy-start.2
  546.7 142.4 %all-to-all-start.4 = ((f32[16,3,256,128]{3,2,1,0:T(8,128)}), f32[16,3,256,128]{3,2,1,0:T(8,128)}, u32[]{:S(2)}, u32[]{:S(2)}) async-start(f32[16,3,256,128]{3,2,1,0:T(8,128)} %get-tuple-element.39), calls=%async_computation.4 | async-start | bytes 12582912 | tf_op jit(solution)/shard_map/all_to_all | solution.py:632
  689.1 97.4 %all-to-all-start.5 = ((f32[16,2,256,128]{3,2,1,0:T(8,128)}), f32[16,2,256,128]{3,2,1,0:T(8,128)}, u32[]{:S(2)}, u32[]{:S(2)}) async-start(f32[16,2,256,128]{3,2,1,0:T(8,128)} %pad_maximum_fusion), calls=%async_computation.5 | async-start | bytes 8388608 | tf_op jit(solution)/shard_map/all_to_all | solution.py:632
  741.9 10.4 %collective-permute-start.2 = (f32[3,256,2048]{2,1,0:T(8,128)}, f32[3,256,2048]{2,1,0:T(8,128)S(1)}, u32[]{:S(2)}, u32[]{:S(2)}) collective-permute-start(f32[3,256,2048]{2,1,0:T(8,128)} %get-tuple-element.44), channel_id=1, source_target_pairs={{0,1},{1,0},{2,3},{3,2},{4,5},{5,4},{6,7},{7,6},{8,9},{9,8},{10,11... | collective-permute-start | bytes 18874376 | tf_op jit(solution)/shard_map/ppermute | solution.py:623
  804.3 4.9 collective-permute-start.3
